TPU v7x, 256 devices: a whole 4x4x8 slice. The times are simulated.
256 devices in a mesh: space: 64 (over x, z, core), slide: 4 (over y).
Axes of the slice: x: 4, y: 4, z: 8, core: 2. Of those that a mesh axis runs over, the one named last changes fastest.
Arguments:
- image: bfloat16 [4, 96, 1024, 128], P('slide', None, 'space'), may hold values from -6 to 6
- cotangent: bfloat16 [4, 96, 1024, 128], P('slide', None, 'space'), may hold values from -6 to 6
- tissue: int32 [4, 64, 8], P('slide', 'space'), may hold values from 0 to 1, as said below
- dw_kernel: float32 [96, 49], replicated, may hold values from -0.875 to 0.875
- dw_bias: float32 [96], replicated, may hold values from -3 to 3
- ln_gain: float32 [96], replicated, may hold values from 0.5 to 1.5
- ln_bias: float32 [96], replicated, may hold values from -2 to 2
- w_in: bfloat16 [96, 384], replicated, may hold values from -0.625 to 0.625
- b_in: float32 [384], replicated, may hold values from -3 to 3
- w_out: bfloat16 [96, 384], replicated, may hold values from -0.3125 to 0.3125
- b_out: float32 [96], replicated, may hold values from -3 to 3
- layer_scale: float32 [96], replicated, may hold values from 0.4 to 1.2
Outputs:
- out_image: bfloat16 [4, 96, 1024, 128], P('slide', None, 'space')
- grad_image: bfloat16 [4, 96, 1024, 128], P('slide', None, 'space')
- grad_mlp: float32 [2, 96, 384], replicated
- grad_kernel: float32 [96, 49], replicated
- grad_vectors: float32 [5, 96], replicated
- grad_b_in: float32 [384], replicated
Inputs may be any that keep to these rules, and one draw needn't show every extreme that they name: In every slide, each of the 8 tiles of one index of space is either tissue or not.
All inputs are finite; a program needn't handle non-finite values.
Results may differ from a plain program's by a relative error of at most 0.007.
Values may be sent and summed in bfloat16 or wider, within the bound.
A program may use at most 64 MiB of HBM per device.

v0:
```python
import math

import jax
import jax.numpy as jnp
from jax import lax
from jax.sharding import PartitionSpec as P

TP = 16
TROWS = 8
TCOL_DEV = 1
MOST = 8


RADIUS = 3
KERNEL_SIDE = 7
EPSILON = 1e-06
GRAD_COEF = 4.0


def extended(block, sides, width):
    for axis, dim in sides:
        count = lax.axis_size(axis)
        forward = [(i, i + 1) for i in range(count - 1)]
        backward = [(target, source) for source, target in forward]
        low = lax.ppermute(
            lax.slice_in_dim(block, block.shape[dim] - width, None, axis=dim), axis, forward
        )
        high = lax.ppermute(lax.slice_in_dim(block, 0, width, axis=dim), axis, backward)
        block = jnp.concatenate([low, block, high], axis=dim)
    return block


def shifted(values, axis, stride, radix, shift):
    pairs = []
    for i in range(lax.axis_size(axis)):
        digit = (i // stride) % radix
        pairs.append((i, i + ((digit + shift) % radix - digit) * stride))
    return lax.ppermute(values, axis, pairs)


def digit_groups(axes):
    groups = []
    for axis in axes:
        stride, size = 1, lax.axis_size(axis)
        while stride < size:
            radix = 4 if size % (stride * 4) == 0 else 2
            groups.append((axis, stride, radix))
            stride *= radix
    return groups


def summed_everywhere(parts, axes, lanes=128, halvings=2):
    flat = jnp.concatenate([p.reshape(-1) for p in parts])
    rows = -(-flat.shape[0] // lanes)
    rows += (-rows) % 128
    block = jnp.pad(flat, (0, rows * lanes - flat.shape[0])).reshape(rows, lanes)
    steps = []
    for number, (axis, stride, radix) in enumerate(digit_groups(axes)):
        digit = (lax.axis_index(axis) // stride) % radix
        height, rest = divmod(block.shape[0], radix)
        if rest or number >= halvings:
            stack = jnp.zeros((radix,) + block.shape, block.dtype)
            stack = lax.dynamic_update_index_in_dim(stack, block, digit, 0)
            for shift in range(1, radix):
                got = shifted(block, axis, stride, radix, shift)
                stack = lax.dynamic_update_index_in_dim(stack, got, (digit - shift) % radix, 0)
            block = stack[0]
            for k in range(1, radix):
                block = block + stack[k]
            continue
        keep = lax.dynamic_slice_in_dim(block, digit * height, height)
        for shift in range(1, radix):
            send = lax.dynamic_slice_in_dim(block, ((digit + shift) % radix) * height, height)
            keep = keep + shifted(send, axis, stride, radix, shift)
        block = keep
        steps.append((axis, stride, radix, digit))
    for axis, stride, radix, digit in reversed(steps):
        height = block.shape[0]
        whole = jnp.zeros((height * radix,) + block.shape[1:], block.dtype)
        whole = lax.dynamic_update_slice_in_dim(whole, block, digit * height, 0)
        for shift in range(1, radix):
            got = shifted(block, axis, stride, radix, shift)
            whole = lax.dynamic_update_slice_in_dim(
                whole, got, ((digit - shift) % radix) * height, 0
            )
        block = whole
    flat = block.reshape(-1)
    out, start = [], 0
    for p in parts:
        out.append(flat[start : start + p.size].reshape(p.shape))
        start += p.size
    return tuple(out)

def rounded(values):
    return lax.optimization_barrier(values.astype(jnp.bfloat16))


def gelu_value(values):
    return 0.5 * values * (1.0 + jax.scipy.special.erf(values * (1.0 / math.sqrt(2.0))))


def gelu_slope(values):
    return 0.5 * (1.0 + jax.scipy.special.erf(values * (1.0 / math.sqrt(2.0)))) + values * jnp.exp(
        -0.5 * values * values
    ) * (1.0 / math.sqrt(2.0 * math.pi))


def depthwise(padded, kernel, strip_w, strip_h):
    result = jnp.zeros((padded.shape[0], strip_w, strip_h), jnp.float32)
    for k_row in range(KERNEL_SIDE):
        for k_col in range(KERNEL_SIDE):
            weight = kernel[:, k_row * KERNEL_SIDE + k_col][:, None, None]
            result = result + weight * padded[
                :, k_row : k_row + strip_w, k_col : k_col + strip_h
            ].astype(jnp.float32)
    return result


def kernel_sums(padded, grad_pre, strip_w, strip_h):
    grad_f = grad_pre.astype(jnp.float32)
    entries = []
    for k_row in range(KERNEL_SIDE):
        for k_col in range(KERNEL_SIDE):
            piece = padded[:, k_row : k_row + strip_w, k_col : k_col + strip_h].astype(jnp.float32)
            entries.append(jnp.sum(grad_f * piece, axis=(1, 2)))
    return jnp.stack(entries, axis=1)


def to_tiles(planes):
    channels = planes.shape[0]
    shaped = planes.reshape(channels, TCOL_DEV, TP, TROWS, TP).transpose(1, 3, 0, 2, 4)
    return shaped.reshape(TCOL_DEV * TROWS, channels, TP * TP)


def from_tiles(tiles_in):
    channels = tiles_in.shape[1]
    shaped = tiles_in.reshape(TCOL_DEV, TROWS, channels, TP, TP).transpose(2, 0, 3, 1, 4)
    return shaped.reshape(channels, TCOL_DEV * TP, TROWS * TP)


def mlp_pixels(w_in, w_out, b_in, b_out, x_pix, d_pix):
    flt = jnp.float32
    pre_act = jnp.einsum("cf,cp->fp", w_in, x_pix, preferred_element_type=flt) + b_in[:, None]
    hidden = rounded(gelu_value(pre_act))
    mlp_out = rounded(
        jnp.einsum("cf,fp->cp", w_out, hidden, preferred_element_type=flt) + b_out[:, None]
    )
    back_hid = jnp.einsum("cf,cp->fp", w_out, d_pix, preferred_element_type=flt)
    grad_act = rounded(back_hid * gelu_slope(pre_act))
    grad_ln = rounded(jnp.einsum("cf,fp->cp", w_in, grad_act, preferred_element_type=flt))
    gw_in = jnp.einsum("cp,fp->cf", x_pix, grad_act, preferred_element_type=flt)
    gw_out = jnp.einsum("cp,fp->cf", d_pix, hidden, preferred_element_type=flt)
    gb_in = jnp.sum(grad_act.astype(flt), axis=1)
    gb_out = jnp.sum(d_pix.astype(flt), axis=1)
    return (mlp_out, grad_ln, gw_in, gw_out, gb_in, gb_out)


def on_device(
    image,
    cotangent,
    tissue,
    dw_kernel,
    dw_bias,
    ln_gain,
    ln_bias,
    w_in,
    b_in,
    w_out,
    b_out,
    layer_scale,
):
    flt = jnp.float32
    strip_w = image.shape[2]
    strip_h = image.shape[3]
    gscale = GRAD_COEF / math.sqrt(
        lax.axis_size("space") * lax.axis_size("slide") * strip_w * strip_h
    )
    live_tiles = tissue[0]
    pixel_mask = jnp.repeat(jnp.repeat(live_tiles, TP, axis=0), TP, axis=1).astype(jnp.bfloat16)
    pix_f = pixel_mask[None].astype(flt)
    masked = image[0] * pixel_mask[None]
    rimmed = extended(masked, (("space", 1),), RADIUS)
    padded = jnp.pad(rimmed, ((0, 0), (0, 0), (RADIUS, RADIUS)))
    pre = depthwise(padded, dw_kernel, strip_w, strip_h) + dw_bias[:, None, None]
    centered = pre - jnp.mean(pre, axis=0, keepdims=True)
    inv_std = lax.rsqrt(jnp.mean(centered * centered, axis=0, keepdims=True) + EPSILON)
    normed = centered * inv_std
    ln_out = rounded(normed * ln_gain[:, None, None] + ln_bias[:, None, None])
    cot_f = cotangent[0].astype(flt)
    grad_mix = rounded(cot_f * pix_f * layer_scale[:, None, None])
    channels, pixels = ln_out.shape[0], strip_w * strip_h
    mo_flat, dxh_flat, gw_in, gw_out, gb_in, gb_out = mlp_pixels(
        w_in, w_out, b_in, b_out, ln_out.reshape(channels, pixels), grad_mix.reshape(channels, pixels)
    )
    mlp_out = mo_flat.reshape(ln_out.shape) * pixel_mask[None]
    grad_ln = dxh_flat.reshape(ln_out.shape) * pixel_mask[None]
    out_image = (
        pix_f * (masked.astype(flt) + layer_scale[:, None, None] * mlp_out.astype(flt))
    ).astype(jnp.bfloat16)
    q_term = grad_ln.astype(flt) * ln_gain[:, None, None]
    grad_pre = rounded(
        inv_std
        * (
            q_term
            - jnp.mean(q_term, axis=0, keepdims=True)
            - normed * jnp.mean(q_term * normed, axis=0, keepdims=True)
        )
    )
    grad_rim = extended(grad_pre, (("space", 1),), RADIUS)
    grad_padded = jnp.pad(grad_rim, ((0, 0), (0, 0), (RADIUS, RADIUS)))
    back_conv = depthwise(grad_padded, dw_kernel[:, ::-1], strip_w, strip_h)
    grad_image = (pix_f * (cot_f + back_conv)).astype(jnp.bfloat16)
    grad_k = kernel_sums(padded, grad_pre, strip_w, strip_h) * gscale
    vectors = (
        jnp.stack(
            [
                jnp.sum(grad_pre.astype(flt), axis=(1, 2)),
                jnp.sum(grad_ln.astype(flt) * normed, axis=(1, 2)),
                jnp.sum(grad_ln.astype(flt), axis=(1, 2)),
                gb_out,
                jnp.sum(cot_f * pix_f * mlp_out.astype(flt), axis=(1, 2)),
            ],
            axis=0,
        )
        * gscale
    )
    local_mlp = jnp.stack([gw_in, gw_out], axis=0) * gscale
    grad_mlp, grad_kernel, grad_vectors, grad_b_in = summed_everywhere(
        (local_mlp, grad_k, vectors, gb_in * gscale), ("space", "slide")
    )
    return (out_image[None], grad_image[None], grad_mlp, grad_kernel, grad_vectors, grad_b_in)


def solution(mesh):
    placed = (
        P("slide", None, "space", None),
        P("slide", None, "space", None),
        P("slide", "space", None),
        P(),
        P(),
        P(),
        P(),
        P(),
        P(),
        P(),
        P(),
        P(),
    )
    return jax.shard_map(
        on_device,
        mesh=mesh,
        in_specs=placed,
        out_specs=(
            P("slide", None, "space", None),
            P("slide", None, "space", None),
            P(),
            P(),
            P(),
            P(),
        ),
        check_vma=False,
    )
```

profile of v0, /device:TPU:3, one launch (start us, length us, event | category | flops | bytes accessed | tf_op | source)
XLA Modules:
  0.0 128.2 jit_solution(6245931398361530641)
XLA Ops:
  0.7 0.7 convert_bitcast_fusion
  1.5 1.0 bitcast_multiply_fusion.5
  2.6 4.1 %collective-permute-start = (bf16[96,3,128]{2,1,0:T(4,128)(2,1)S(1)}, bf16[96,3,128]{2,1,0:T(4,128)(2,1)S(1)}, u32[]{:S(2)}, u32[]{:S(2)}) collective-permute-start(bf16[96,3,128]{2,1,0:T(4,128)(2,1)S(1)} %get-tuple-element.80), channel_id=1, source_target_pairs={{0,4},{4,8},{8,12},{12,16},{16,20},{20,24},{24,28},{28,32},{32,36}... | collective-permute-start | bytes 221192 | tf_op jit(solution)/shard_map/ppermute | solution.py:25
  6.8 1.9 %collective-permute-start.1 = (bf16[96,3,128]{2,1,0:T(4,128)(2,1)S(1)}, bf16[96,3,128]{2,1,0:T(4,128)(2,1)S(1)}, u32[]{:S(2)}, u32[]{:S(2)}) collective-permute-start(bf16[96,3,128]{2,1,0:T(4,128)(2,1)S(1)} %get-tuple-element.81), channel_id=1, source_target_pairs={{4,0},{8,4},{12,8},{16,12},{20,16},{24,20},{28,24},{32,28},{36,32}... | collective-permute-start | bytes 221192 | tf_op jit(solution)/shard_map/ppermute | solution.py:28
  8.7 1.0 slice_bitcast_fusion.48
  9.7 1.0 slice_bitcast_fusion.47
  10.7 0.9 slice_bitcast_fusion.46
  11.7 1.2 fusion.19
  12.9 0.8 convert_reduce_fusion.3
  13.7 1.0 select_maximum_fusion.2
  14.8 11.6 %fusion.171 = (f32[16,128]{1,0:T(8,128)S(1)}, f32[96,16,128]{2,1,0:T(8,128)S(1)}) fusion(f32[96]{0:T(128)S(1)} %copy-done.7, bf16[96,22,134]{2,1,0:T(8,128)(2,1)S(1)} %select_maximum_fusion.2, f32[96]{0:T(128)S(1)} %get-tuple-element.135, f32[96]{0:T(128)S(1)} %get-tuple-element.136, f32[96]{0:T(128)S(1)} %get-tuple-element.89, ...), kind=kLoop, calls=%fused_computation.410 | loop fusion | flops 32634880 | bytes 17869568 | tf_op jit(solution)/shard_map/reduce_sum | solution.py:185
  26.9 1.0 fusion.7
  27.8 1.6 %fusion.5 = bf16[384,2048]{0,1:T(8,128)(2,1)S(1)} fusion(f32[2048,384]{1,0:T(8,128)S(1)} %get-tuple-element.138, bf16[96,384]{1,0:T(8,128)(2,1)S(1)} %copy-done.3, bf16[12,8,16,128]{3,2,1,0:T(8,128)(2,1)S(1)} %bitcast.259), kind=kOutput, calls=%fused_computation.59 | convolution fusion | flops 158859264 | bytes 5185536 | tf_op jit(solution)/shard_map/cf,cp->fp/dot_general | solution.py:148
  30.9 1.2 fusion.73
  32.6 7.6 %fusion.149 = (f32[96]{0:T(128)S(1)}, f32[96]{0:T(128)S(1)}, f32[96]{0:T(128)S(1)}, f32[96]{0:T(128)S(1)}, f32[96]{0:T(128)S(1)}, /*index=5*/f32[96]{0:T(128)S(1...) fusion(bf16[96,16,128]{2,1,0:T(8,128)(2,1)S(1)} %fusion.23, ...), kind=kLoop, calls=%fused_computation.270 | loop fusion | flops 10811712 | bytes 7478016 | tf_op jit(solution)/shard_map/reduce_sum | solution.py:125
  40.2 7.6 %fusion.150 = (f32[96]{0:T(128)S(1)}, f32[96]{0:T(128)S(1)}, f32[96]{0:T(128)S(1)}, f32[96]{0:T(128)S(1)}, f32[96]{0:T(128)S(1)}, /*index=5*/f32[96]{0:T(128)S(1...) fusion(bf16[96,16,128]{2,1,0:T(8,128)(2,1)S(1)} %fusion.23, ...), kind=kLoop, calls=%fused_computation.271 | loop fusion | flops 10811712 | bytes 7478016 | tf_op jit(solution)/shard_map/reduce_sum | solution.py:125
  47.8 2.1 %fusion.148 = (f32[96]{0:T(128)S(1)}, f32[96]{0:T(128)S(1)}, f32[96]{0:T(128)S(1)}, f32[96]{0:T(128)S(1)}, f32[96]{0:T(128)S(1)}, /*index=5*/f32[96]{0:T(128)S(1)}) fusion(bf16[96,16,128]{2,1,0:T(8,128)(2,1)S(1)} %fusion.23, bf16[96,22,134]{2,1,0:T(8,128)(2,1)S(1)} %select_maximum_fusion.2), kind=kLoop, calls=%fused_computation.269 | loop fusion | flops 3734976 | bytes 2754816 | tf_op jit(solution)/shard_map/reduce_sum | solution.py:125
  51.1 2.3 %fusion.147 = (f32[96]{0:T(128)S(1)}, f32[96]{0:T(128)S(1)}, f32[96]{0:T(128)S(1)}, f32[96]{0:T(128)S(1)}, f32[96]{0:T(128)S(1)}, /*index=5*/f32[96]{0:T(128)S(1)}, f32[96]{0:T(128)S(1)}, f32[96]{0:T(128)S(1)}) fusion(bf16[96,16,128]{2,1,0:T(8,128)(2,1)S(1)} %fusion.23, bf16[96,3,128]{2,1,0:T(4,128)(2,1)S(1)} %collective-permute-done.1, ...), kind=kLoop, calls=%fused_computation.268 | loop fusion | flops 8060160 | bytes 936960 | tf_op jit(solution)/shard_map/reduce_sum | solution.py:125
  54.0 1.4 %concatenate.35 = f32[79296]{0:T(1024)S(1)} concatenate(f32[73728]{0:T(1024)S(1)} %mul.1432, f32[4704]{0:T(1024)S(1)} %mul.1484, f32[480]{0:T(512)S(1)} %mul.1490, f32[384]{0:T(512)S(1)} %broadcast_multiply_fusion.4), dimensions={0} | concatenate | bytes 634368 | tf_op jit(solution)/shard_map/concatenate | solution.py:53
  55.5 1.8 %collective-permute-start.4 = (f32[160,128]{1,0:T(8,128)S(1)}, f32[160,128]{1,0:T(8,128)S(1)}, u32[]{:S(2)}, u32[]{:S(2)}) collective-permute-start(f32[160,128]{1,0:T(8,128)S(1)} %get-tuple-element.82), channel_id=1, source_target_pairs={{0,4},{4,8},{8,12},{12,0},{16,20},{20,24},{24,28},{28,16},{32,36},... | collective-permute-start | bytes 245768 | tf_op jit(solution)/shard_map/ppermute | solution.py:38
  57.3 3.4 %collective-permute-start.5 = (f32[160,128]{1,0:T(8,128)S(1)}, f32[160,128]{1,0:T(8,128)S(1)}, u32[]{:S(2)}, u32[]{:S(2)}) collective-permute-start(f32[160,128]{1,0:T(8,128)S(1)} %get-tuple-element.84), channel_id=1, source_target_pairs={{0,8},{4,12},{8,0},{12,4},{16,24},{20,28},{24,16},{28,20},{32,40},... | collective-permute-start | bytes 245768 | tf_op jit(solution)/shard_map/ppermute | solution.py:38
  60.7 3.8 %collective-permute-done.5 = f32[160,128]{1,0:T(8,128)S(1)} collective-permute-done((f32[160,128]{1,0:T(8,128)S(1)}, f32[160,128]{1,0:T(8,128)S(1)}, u32[]{:S(2)}, u32[]{:S(2)}) %collective-permute-start.5) | collective-permute-done | bytes 81952 | tf_op jit(solution)/shard_map/ppermute | solution.py:38
  64.4 0.7 collective-permute-done.6
  65.2 1.0 collective-permute-start.7
  66.2 3.7 %collective-permute-start.8 = (f32[40,128]{1,0:T(8,128)S(1)}, f32[40,128]{1,0:T(8,128)S(1)}, u32[]{:S(2)}, u32[]{:S(2)}) collective-permute-start(f32[40,128]{1,0:T(8,128)S(1)} %get-tuple-element.87), channel_id=1, source_target_pairs={{0,32},{4,36},{8,40},{12,44},{16,48},{20,52},{24,56},{28,60},{32,0... | collective-permute-start | bytes 61448 | tf_op jit(solution)/shard_map/ppermute | solution.py:38
  69.9 3.5 %collective-permute-start.9 = (f32[40,128]{1,0:T(8,128)S(1)}, f32[40,128]{1,0:T(8,128)S(1)}, u32[]{:S(2)}, u32[]{:S(2)}) collective-permute-start(f32[40,128]{1,0:T(8,128)S(1)} %get-tuple-element.86), channel_id=1, source_target_pairs={{0,48},{4,52},{8,56},{12,60},{16,0},{20,4},{24,8},{28,12},{32,16},... | collective-permute-start | bytes 61448 | tf_op jit(solution)/shard_map/ppermute | solution.py:38
  73.5 2.6 %collective-permute-start.2 = (bf16[96,3,128]{2,1,0:T(4,128)(2,1)S(1)}, bf16[96,3,128]{2,1,0:T(4,128)(2,1)S(1)}, u32[]{:S(2)}, u32[]{:S(2)}) collective-permute-start(bf16[96,3,128]{2,1,0:T(4,128)(2,1)S(1)} %get-tuple-element.78), channel_id=1, source_target_pairs={{0,4},{4,8},{8,12},{12,16},{16,20},{20,24},{24,28},{28,32},{32,36}... | collective-permute-start | bytes 221192 | tf_op jit(solution)/shard_map/ppermute | solution.py:25
  76.1 1.9 %collective-permute-start.3 = (bf16[96,3,128]{2,1,0:T(4,128)(2,1)S(1)}, bf16[96,3,128]{2,1,0:T(4,128)(2,1)S(1)}, u32[]{:S(2)}, u32[]{:S(2)}) collective-permute-start(bf16[96,3,128]{2,1,0:T(4,128)(2,1)S(1)} %get-tuple-element.79), channel_id=1, source_target_pairs={{4,0},{8,4},{12,8},{16,12},{20,16},{24,20},{28,24},{32,28},{36,32}... | collective-permute-start | bytes 221192 | tf_op jit(solution)/shard_map/ppermute | solution.py:28
  78.1 1.3 %collective-permute-start.10 = (f32[40,128]{1,0:T(8,128)S(1)}, f32[40,128]{1,0:T(8,128)S(1)}, u32[]{:S(2)}, u32[]{:S(2)}) collective-permute-start(f32[40,128]{1,0:T(8,128)S(1)} %get-tuple-element.75), channel_id=1, source_target_pairs={{0,64},{4,68},{8,72},{12,76},{16,80},{20,84},{24,88},{28,92},{32,9... | collective-permute-start | bytes 61448 | tf_op jit(solution)/shard_map/ppermute | solution.py:38
  79.4 1.0 multiply_convert_fusion
  80.4 0.8 collective-permute-start.11
  81.2 1.9 %collective-permute-start.12 = (f32[40,128]{1,0:T(8,128)S(1)}, f32[40,128]{1,0:T(8,128)S(1)}, u32[]{:S(2)}, u32[]{:S(2)}) collective-permute-start(f32[40,128]{1,0:T(8,128)S(1)} %get-tuple-element.75), channel_id=1, source_target_pairs={{0,192},{4,196},{8,200},{12,204},{16,208},{20,212},{24,216},{28,22... | collective-permute-start | bytes 61448 | tf_op jit(solution)/shard_map/ppermute | solution.py:38
  83.1 1.4 %collective-permute-done.11 = f32[40,128]{1,0:T(8,128)S(1)} collective-permute-done((f32[40,128]{1,0:T(8,128)S(1)}, f32[40,128]{1,0:T(8,128)S(1)}, u32[]{:S(2)}, u32[]{:S(2)}) %collective-permute-start.11) | collective-permute-done | bytes 20512 | tf_op jit(solution)/shard_map/ppermute | solution.py:38
  84.6 1.4 %collective-permute-start.13 = (f32[40,128]{1,0:T(8,128)S(1)}, f32[40,128]{1,0:T(8,128)S(1)}, u32[]{:S(2)}, u32[]{:S(2)}) collective-permute-start(f32[40,128]{1,0:T(8,128)S(1)} %bitcast.269), channel_id=1, source_target_pairs={{0,1},{1,2},{2,3},{3,0},{4,5},{5,6},{6,7},{7,4},{8,9},{9,10},{10,1... | collective-permute-start | bytes 61448 | tf_op jit(solution)/shard_map/ppermute | solution.py:38
  86.0 1.0 select_maximum_fusion
  87.0 2.7 %collective-permute-start.14 = (f32[40,128]{1,0:T(8,128)S(1)}, f32[40,128]{1,0:T(8,128)S(1)}, u32[]{:S(2)}, u32[]{:S(2)}) collective-permute-start(f32[40,128]{1,0:T(8,128)S(1)} %bitcast.270), channel_id=1, source_target_pairs={{0,2},{1,3},{2,0},{3,1},{4,6},{5,7},{6,4},{7,5},{8,10},{9,11},{10,... | collective-permute-start | bytes 61448 | tf_op jit(solution)/shard_map/ppermute | solution.py:38
  89.7 1.1 collective-permute-start.15
  91.2 1.1 collective-permute-done.15
  92.5 11.9 %fusion.164 = bf16[1,96,16,128]{3,2,1,0:T(8,128)(2,1)} fusion(bf16[96,22,134]{2,1,0:T(8,128)(2,1)S(1)} %select_maximum_fusion, f32[96]{0:T(128)S(1)} %get-tuple-element.88, f32[96]{0:T(128)S(1)} %get-tuple-element.107, f32[96]{0:T(128)S(1)} %get-tuple-element.126, bf16[96,3,128]{2,1,0:T(4,128)(2,1)S(1)} %collective-permute-done.3, ...), kind=kLoop, calls=%fused_computation.314 | loop fusion | flops 33030144 | bytes 17861504 | tf_op jit(solution)/shard_map/broadcast_in_dim | solution.py:231
  104.4 2.0 %collective-permute-start.17 = (f32[40,128]{1,0:T(8,128)S(1)}, f32[40,128]{1,0:T(8,128)S(1)}, u32[]{:S(2)}, u32[]{:S(2)}) collective-permute-start(f32[40,128]{1,0:T(8,128)S(1)} %get-tuple-element.71), channel_id=1, source_target_pairs={{0,32},{4,36},{8,40},{12,44},{16,48},{20,52},{24,56},{28,60},{32,0... | collective-permute-start | bytes 61448 | tf_op jit(solution)/shard_map/ppermute | solution.py:38
  106.4 2.2 %collective-permute-start.18 = (f32[40,128]{1,0:T(8,128)S(1)}, f32[40,128]{1,0:T(8,128)S(1)}, u32[]{:S(2)}, u32[]{:S(2)}) collective-permute-start(f32[40,128]{1,0:T(8,128)S(1)} %get-tuple-element.71), channel_id=1, source_target_pairs={{0,48},{4,52},{8,56},{12,60},{16,0},{20,4},{24,8},{28,12},{32,16},... | collective-permute-start | bytes 61448 | tf_op jit(solution)/shard_map/ppermute | solution.py:38
  108.6 2.3 %collective-permute-done.17 = f32[40,128]{1,0:T(8,128)S(1)} collective-permute-done((f32[40,128]{1,0:T(8,128)S(1)}, f32[40,128]{1,0:T(8,128)S(1)}, u32[]{:S(2)}, u32[]{:S(2)}) %collective-permute-start.17) | collective-permute-done | bytes 20512 | tf_op jit(solution)/shard_map/ppermute | solution.py:38
  111.1 6.5 %collective-permute-start.19 = (f32[160,128]{1,0:T(8,128)S(1)}, f32[160,128]{1,0:T(8,128)S(1)}, u32[]{:S(2)}, u32[]{:S(2)}) collective-permute-start(f32[160,128]{1,0:T(8,128)S(1)} %constant_dynamic-update-slice_fusion.4), channel_id=1, source_target_pairs={{0,4},{4,8},{8,12},{12,0},{16,20},{20,24},{24,28},{28,16},{32,36},... | collective-permute-start | bytes 245768 | tf_op jit(solution)/shard_map/ppermute | solution.py:38
  117.6 3.0 %collective-permute-start.20 = (f32[160,128]{1,0:T(8,128)S(1)}, f32[160,128]{1,0:T(8,128)S(1)}, u32[]{:S(2)}, u32[]{:S(2)}) collective-permute-start(f32[160,128]{1,0:T(8,128)S(1)} %constant_dynamic-update-slice_fusion.4), channel_id=1, source_target_pairs={{0,8},{4,12},{8,0},{12,4},{16,24},{20,28},{24,16},{28,20},{32,40},... | collective-permute-start | bytes 245768 | tf_op jit(solution)/shard_map/ppermute | solution.py:38
  120.7 3.8 %collective-permute-done.20 = f32[160,128]{1,0:T(8,128)S(1)} collective-permute-done((f32[160,128]{1,0:T(8,128)S(1)}, f32[160,128]{1,0:T(8,128)S(1)}, u32[]{:S(2)}, u32[]{:S(2)}) %collective-permute-start.20) | collective-permute-done | bytes 81952 | tf_op jit(solution)/shard_map/ppermute | solution.py:38
  125.8 0.8 reshape.228
  126.8 0.7 copy.19
  127.5 0.7 reshape.231
  (99 shorter events, 6.8 us)
Async XLA Ops:
  0.6 26.2 %copy-start = (bf16[96,384]{1,0:T(8,128)(2,1)S(1)}, bf16[96,384]{1,0:T(8,128)(2,1)}, u32[]{:S(2)}) copy-start(bf16[96,384]{1,0:T(8,128)(2,1)} %param.19) | copy-start | bytes 221188
  0.6 14.1 %copy-start.7 = (f32[96]{0:T(128)S(1)}, f32[96]{0:T(128)}, u32[]{:S(2)}) copy-start(f32[96]{0:T(128)} %param.16) | copy-start | bytes 1156
  2.6 11.1 %collective-permute-start = (bf16[96,3,128]{2,1,0:T(4,128)(2,1)S(1)}, bf16[96,3,128]{2,1,0:T(4,128)(2,1)S(1)}, u32[]{:S(2)}, u32[]{:S(2)}) collective-permute-start(bf16[96,3,128]{2,1,0:T(4,128)(2,1)S(1)} %get-tuple-element.80), channel_id=1, source_target_pairs={{0,4},{4,8},{8,12},{12,16},{16,20},{20,24},{24,28},{28,32},{32,36}... | collective-permute-start | bytes 221192 | tf_op jit(solution)/shard_map/ppermute | solution.py:25
  6.8 7.0 %collective-permute-start.1 = (bf16[96,3,128]{2,1,0:T(4,128)(2,1)S(1)}, bf16[96,3,128]{2,1,0:T(4,128)(2,1)S(1)}, u32[]{:S(2)}, u32[]{:S(2)}) collective-permute-start(bf16[96,3,128]{2,1,0:T(4,128)(2,1)S(1)} %get-tuple-element.81), channel_id=1, source_target_pairs={{4,0},{8,4},{12,8},{16,12},{20,16},{24,20},{28,24},{32,28},{36,32}... | collective-permute-start | bytes 221192 | tf_op jit(solution)/shard_map/ppermute | solution.py:28
  14.8 11.8 %copy-start.4 = (f32[96]{0:T(128)S(1)}, f32[96]{0:T(128)}, u32[]{:S(2)}) copy-start(f32[96]{0:T(128)} %param.17) | copy-start | bytes 1156
  14.8 11.7 %copy-start.8 = (f32[96]{0:T(128)S(1)}, f32[96]{0:T(128)}, u32[]{:S(2)}) copy-start(f32[96]{0:T(128)} %param.18) | copy-start | bytes 1156
  14.8 12.0 %copy-start.6 = (f32[384]{0:T(512)S(1)}, f32[384]{0:T(512)}, u32[]{:S(2)}) copy-start(f32[384]{0:T(512)} %param.20) | copy-start | bytes 4612
  26.8 1.0 copy-start.3
  29.5 0.7 copy-start.9
  29.5 1.4 %copy-start.1 = (bf16[1,96,16,128]{3,2,1,0:T(8,128)(2,1)S(1)}, bf16[1,96,16,128]{3,2,1,0:T(8,128)(2,1)}, u32[]{:S(2)}) copy-start(bf16[1,96,16,128]{3,2,1,0:T(8,128)(2,1)} %param.13) | copy-start | bytes 1179652
  53.9 25.5 %copy-start.2 = (bf16[1,96,16,128]{3,2,1,0:T(8,128)(2,1)S(1)}, bf16[1,96,16,128]{3,2,1,0:T(8,128)(2,1)}, u32[]{:S(2)}) copy-start(bf16[1,96,16,128]{3,2,1,0:T(8,128)(2,1)} %param.12) | copy-start | bytes 1179652
  53.9 25.4 %copy-start.5 = (f32[96]{0:T(128)S(1)}, f32[96]{0:T(128)}, u32[]{:S(2)}) copy-start(f32[96]{0:T(128)} %param.23) | copy-start | bytes 1156
  55.5 5.2 %collective-permute-start.4 = (f32[160,128]{1,0:T(8,128)S(1)}, f32[160,128]{1,0:T(8,128)S(1)}, u32[]{:S(2)}, u32[]{:S(2)}) collective-permute-start(f32[160,128]{1,0:T(8,128)S(1)} %get-tuple-element.82), channel_id=1, source_target_pairs={{0,4},{4,8},{8,12},{12,0},{16,20},{20,24},{24,28},{28,16},{32,36},... | collective-permute-start | bytes 245768 | tf_op jit(solution)/shard_map/ppermute | solution.py:38
  57.3 7.1 %collective-permute-start.5 = (f32[160,128]{1,0:T(8,128)S(1)}, f32[160,128]{1,0:T(8,128)S(1)}, u32[]{:S(2)}, u32[]{:S(2)}) collective-permute-start(f32[160,128]{1,0:T(8,128)S(1)} %get-tuple-element.84), channel_id=1, source_target_pairs={{0,8},{4,12},{8,0},{12,4},{16,24},{20,28},{24,16},{28,20},{32,40},... | collective-permute-start | bytes 245768 | tf_op jit(solution)/shard_map/ppermute | solution.py:38
  60.7 4.5 %collective-permute-start.6 = (f32[160,128]{1,0:T(8,128)S(1)}, f32[160,128]{1,0:T(8,128)S(1)}, u32[]{:S(2)}, u32[]{:S(2)}) collective-permute-start(f32[160,128]{1,0:T(8,128)S(1)} %get-tuple-element.83), channel_id=1, source_target_pairs={{0,12},{4,0},{8,4},{12,8},{16,28},{20,16},{24,20},{28,24},{32,44},... | collective-permute-start | bytes 245768 | tf_op jit(solution)/shard_map/ppermute | solution.py:38
  65.2 12.8 %collective-permute-start.7 = (f32[40,128]{1,0:T(8,128)S(1)}, f32[40,128]{1,0:T(8,128)S(1)}, u32[]{:S(2)}, u32[]{:S(2)}) collective-permute-start(f32[40,128]{1,0:T(8,128)S(1)} %get-tuple-element.85), channel_id=1, source_target_pairs={{0,16},{4,20},{8,24},{12,28},{16,32},{20,36},{24,40},{28,44},{32,4... | collective-permute-start | bytes 61448 | tf_op jit(solution)/shard_map/ppermute | solution.py:38
  66.2 11.8 %collective-permute-start.8 = (f32[40,128]{1,0:T(8,128)S(1)}, f32[40,128]{1,0:T(8,128)S(1)}, u32[]{:S(2)}, u32[]{:S(2)}) collective-permute-start(f32[40,128]{1,0:T(8,128)S(1)} %get-tuple-element.87), channel_id=1, source_target_pairs={{0,32},{4,36},{8,40},{12,44},{16,48},{20,52},{24,56},{28,60},{32,0... | collective-permute-start | bytes 61448 | tf_op jit(solution)/shard_map/ppermute | solution.py:38
  69.9 8.1 %collective-permute-start.9 = (f32[40,128]{1,0:T(8,128)S(1)}, f32[40,128]{1,0:T(8,128)S(1)}, u32[]{:S(2)}, u32[]{:S(2)}) collective-permute-start(f32[40,128]{1,0:T(8,128)S(1)} %get-tuple-element.86), channel_id=1, source_target_pairs={{0,48},{4,52},{8,56},{12,60},{16,0},{20,4},{24,8},{28,12},{32,16},... | collective-permute-start | bytes 61448 | tf_op jit(solution)/shard_map/ppermute | solution.py:38
  73.5 12.5 %collective-permute-start.2 = (bf16[96,3,128]{2,1,0:T(4,128)(2,1)S(1)}, bf16[96,3,128]{2,1,0:T(4,128)(2,1)S(1)}, u32[]{:S(2)}, u32[]{:S(2)}) collective-permute-start(bf16[96,3,128]{2,1,0:T(4,128)(2,1)S(1)} %get-tuple-element.78), channel_id=1, source_target_pairs={{0,4},{4,8},{8,12},{12,16},{16,20},{20,24},{24,28},{28,32},{32,36}... | collective-permute-start | bytes 221192 | tf_op jit(solution)/shard_map/ppermute | solution.py:25
  76.1 9.9 %collective-permute-start.3 = (bf16[96,3,128]{2,1,0:T(4,128)(2,1)S(1)}, bf16[96,3,128]{2,1,0:T(4,128)(2,1)S(1)}, u32[]{:S(2)}, u32[]{:S(2)}) collective-permute-start(bf16[96,3,128]{2,1,0:T(4,128)(2,1)S(1)} %get-tuple-element.79), channel_id=1, source_target_pairs={{4,0},{8,4},{12,8},{16,12},{20,16},{24,20},{28,24},{32,28},{36,32}... | collective-permute-start | bytes 221192 | tf_op jit(solution)/shard_map/ppermute | solution.py:28
  78.1 5.0 %collective-permute-start.10 = (f32[40,128]{1,0:T(8,128)S(1)}, f32[40,128]{1,0:T(8,128)S(1)}, u32[]{:S(2)}, u32[]{:S(2)}) collective-permute-start(f32[40,128]{1,0:T(8,128)S(1)} %get-tuple-element.75), channel_id=1, source_target_pairs={{0,64},{4,68},{8,72},{12,76},{16,80},{20,84},{24,88},{28,92},{32,9... | collective-permute-start | bytes 61448 | tf_op jit(solution)/shard_map/ppermute | solution.py:38
  80.4 4.1 %collective-permute-start.11 = (f32[40,128]{1,0:T(8,128)S(1)}, f32[40,128]{1,0:T(8,128)S(1)}, u32[]{:S(2)}, u32[]{:S(2)}) collective-permute-start(f32[40,128]{1,0:T(8,128)S(1)} %get-tuple-element.75), channel_id=1, source_target_pairs={{0,128},{4,132},{8,136},{12,140},{16,144},{20,148},{24,152},{28,15... | collective-permute-start | bytes 61448 | tf_op jit(solution)/shard_map/ppermute | solution.py:38
  81.2 3.3 %collective-permute-start.12 = (f32[40,128]{1,0:T(8,128)S(1)}, f32[40,128]{1,0:T(8,128)S(1)}, u32[]{:S(2)}, u32[]{:S(2)}) collective-permute-start(f32[40,128]{1,0:T(8,128)S(1)} %get-tuple-element.75), channel_id=1, source_target_pairs={{0,192},{4,196},{8,200},{12,204},{16,208},{20,212},{24,216},{28,22... | collective-permute-start | bytes 61448 | tf_op jit(solution)/shard_map/ppermute | solution.py:38
  84.6 6.2 %collective-permute-start.13 = (f32[40,128]{1,0:T(8,128)S(1)}, f32[40,128]{1,0:T(8,128)S(1)}, u32[]{:S(2)}, u32[]{:S(2)}) collective-permute-start(f32[40,128]{1,0:T(8,128)S(1)} %bitcast.269), channel_id=1, source_target_pairs={{0,1},{1,2},{2,3},{3,0},{4,5},{5,6},{6,7},{7,4},{8,9},{9,10},{10,1... | collective-permute-start | bytes 61448 | tf_op jit(solution)/shard_map/ppermute | solution.py:38
  87.0 4.2 %collective-permute-start.14 = (f32[40,128]{1,0:T(8,128)S(1)}, f32[40,128]{1,0:T(8,128)S(1)}, u32[]{:S(2)}, u32[]{:S(2)}) collective-permute-start(f32[40,128]{1,0:T(8,128)S(1)} %bitcast.270), channel_id=1, source_target_pairs={{0,2},{1,3},{2,0},{3,1},{4,6},{5,7},{6,4},{7,5},{8,10},{9,11},{10,... | collective-permute-start | bytes 61448 | tf_op jit(solution)/shard_map/ppermute | solution.py:38
  89.7 2.6 %collective-permute-start.15 = (f32[40,128]{1,0:T(8,128)S(1)}, f32[40,128]{1,0:T(8,128)S(1)}, u32[]{:S(2)}, u32[]{:S(2)}) collective-permute-start(f32[40,128]{1,0:T(8,128)S(1)} %bitcast.271), channel_id=1, source_target_pairs={{0,3},{1,0},{2,1},{3,2},{4,7},{5,4},{6,5},{7,6},{8,11},{9,8},{10,9... | collective-permute-start | bytes 61448 | tf_op jit(solution)/shard_map/ppermute | solution.py:38
  92.4 16.2 %collective-permute-start.16 = (f32[40,128]{1,0:T(8,128)S(1)}, f32[40,128]{1,0:T(8,128)S(1)}, u32[]{:S(2)}, u32[]{:S(2)}) collective-permute-start(f32[40,128]{1,0:T(8,128)S(1)} %get-tuple-element.71), channel_id=1, source_target_pairs={{0,16},{4,20},{8,24},{12,28},{16,32},{20,36},{24,40},{28,44},{32,4... | collective-permute-start | bytes 61448 | tf_op jit(solution)/shard_map/ppermute | solution.py:38
  104.4 6.5 %collective-permute-start.17 = (f32[40,128]{1,0:T(8,128)S(1)}, f32[40,128]{1,0:T(8,128)S(1)}, u32[]{:S(2)}, u32[]{:S(2)}) collective-permute-start(f32[40,128]{1,0:T(8,128)S(1)} %get-tuple-element.71), channel_id=1, source_target_pairs={{0,32},{4,36},{8,40},{12,44},{16,48},{20,52},{24,56},{28,60},{32,0... | collective-permute-start | bytes 61448 | tf_op jit(solution)/shard_map/ppermute | solution.py:38
  106.4 4.7 %collective-permute-start.18 = (f32[40,128]{1,0:T(8,128)S(1)}, f32[40,128]{1,0:T(8,128)S(1)}, u32[]{:S(2)}, u32[]{:S(2)}) collective-permute-start(f32[40,128]{1,0:T(8,128)S(1)} %get-tuple-element.71), channel_id=1, source_target_pairs={{0,48},{4,52},{8,56},{12,60},{16,0},{20,4},{24,8},{28,12},{32,16},... | collective-permute-start | bytes 61448 | tf_op jit(solution)/shard_map/ppermute | solution.py:38
  111.1 9.6 %collective-permute-start.19 = (f32[160,128]{1,0:T(8,128)S(1)}, f32[160,128]{1,0:T(8,128)S(1)}, u32[]{:S(2)}, u32[]{:S(2)}) collective-permute-start(f32[160,128]{1,0:T(8,128)S(1)} %constant_dynamic-update-slice_fusion.4), channel_id=1, source_target_pairs={{0,4},{4,8},{8,12},{12,0},{16,20},{20,24},{24,28},{28,16},{32,36},... | collective-permute-start | bytes 245768 | tf_op jit(solution)/shard_map/ppermute | solution.py:38
  117.6 6.9 %collective-permute-start.20 = (f32[160,128]{1,0:T(8,128)S(1)}, f32[160,128]{1,0:T(8,128)S(1)}, u32[]{:S(2)}, u32[]{:S(2)}) collective-permute-start(f32[160,128]{1,0:T(8,128)S(1)} %constant_dynamic-update-slice_fusion.4), channel_id=1, source_target_pairs={{0,8},{4,12},{8,0},{12,4},{16,24},{20,28},{24,16},{28,20},{32,40},... | collective-permute-start | bytes 245768 | tf_op jit(solution)/shard_map/ppermute | solution.py:38
  120.6 4.5 %collective-permute-start.21 = (f32[160,128]{1,0:T(8,128)S(1)}, f32[160,128]{1,0:T(8,128)S(1)}, u32[]{:S(2)}, u32[]{:S(2)}) collective-permute-start(f32[160,128]{1,0:T(8,128)S(1)} %constant_dynamic-update-slice_fusion.4), channel_id=1, source_target_pairs={{0,12},{4,0},{8,4},{12,8},{16,28},{20,16},{24,20},{28,24},{32,44},... | collective-permute-start | bytes 245768 | tf_op jit(solution)/shard_map/ppermute | solution.py:38
where the time goes:
time: 131 us; the launch traced here: 128 us
  other arithmetic  52.4 us (40%)
  starting transfers between devices  46.9 us (36%)
  waiting for transfers between devices  14.3 us (11%)
  local copies, waits for them, and re-layouts  8.65 us (7%)
  matrix products  4.65 us (4%)
    ppermute x18, starting transfers between devices, shifted(): return lax.ppermute(values, axis, pairs)  36.4 us
    reduce_sum x4, other arithmetic, kernel_sums(): entries.append(jnp.sum(grad_f * piece, axis=(1, 2)))  19.6 us
    ppermute x18, waiting for transfers between devices, shifted(): return lax.ppermute(values, axis, pairs)  14.3 us
    broadcast_in_dim x1, other arithmetic, on_device(): grad_image[None]  11.9 us
    reduce_sum x1, other arithmetic, on_device(): centered = pre - jnp.mean(pre, axis=0, keepdims=True)  11.6 us
    ppermute x2, starting transfers between devices, extended(): lax.ppermute(lax.slice_in_dim(block, block.shape[dim] - width, None, axis...  6.69 us
    ppermute x2, starting transfers between devices, extended(): lax.ppermute(lax.slice_in_dim(block, 0, width, axis=dim), axis, backward)  3.84 us
    mul x3, local copies, waits for them, and re-layouts, depthwise(): weight * padded[:, k_row:k_row + strip_w, k_col:k_col + strip_h].astype(j...  2.93 us
  transfers between devices with their start and end apart: 22, of which 9 were waited for; matrix products, arithmetic and copies ran while one was open for 15% of the time, Pallas kernels for 0%

commit v1 on v0

--- a/solution.py
+++ b/solution.py
@@ -49,7 +49,7 @@
     return groups
 
 
-def summed_everywhere(parts, axes, lanes=128, halvings=2):
+def summed_everywhere(parts, axes, lanes=128, halvings=1):
     flat = jnp.concatenate([p.reshape(-1) for p in parts])
     rows = -(-flat.shape[0] // lanes)
     rows += (-rows) % 128

time: 131 us -> 126 us (0.962); the launches traced: 128 us -> 125 us
  starting transfers between devices: 46.9 us -> 37.8 us
  waiting for transfers between devices: 14.3 us -> 20.4 us
    ppermute x18 -> x15, starting transfers between devices: 36.4 us -> 27.2 us  [shifted(): return lax.ppermute(values, axis, pairs)]
    ppermute x18 -> x15, waiting for transfers between devices: 14.3 us -> 20.4 us  [shifted(): return lax.ppermute(values, axis, pairs)]
  transfers between devices with their start and end apart: 22 -> 19, of which waited for: 9 -> 10; matrix products, arithmetic and copies ran while one was open for 15% -> 15% of each run, Pallas kernels for 0% -> 0%
where the time goes in v1:
time: 126 us; the launch traced here: 125 us
  other arithmetic  52.3 us (42%)
  starting transfers between devices  37.8 us (30%)
  waiting for transfers between devices  20.4 us (16%)
  local copies, waits for them, and re-layouts  8.73 us (7%)
  matrix products  4.65 us (4%)
    ppermute x15, starting transfers between devices, shifted(): return lax.ppermute(values, axis, pairs)  27.2 us
    ppermute x15, waiting for transfers between devices, shifted(): return lax.ppermute(values, axis, pairs)  20.4 us
    reduce_sum x4, other arithmetic, kernel_sums(): entries.append(jnp.sum(grad_f * piece, axis=(1, 2)))  19.6 us
    broadcast_in_dim x1, other arithmetic, on_device(): grad_image[None]  11.8 us
    reduce_sum x1, other arithmetic, on_device(): centered = pre - jnp.mean(pre, axis=0, keepdims=True)  11.6 us
    ppermute x2, starting transfers between devices, extended(): lax.ppermute(lax.slice_in_dim(block, block.shape[dim] - width, None, axis...  6.68 us
    ppermute x2, starting transfers between devices, extended(): lax.ppermute(lax.slice_in_dim(block, 0, width, axis=dim), axis, backward)  3.84 us
    mul x3, local copies, waits for them, and re-layouts, depthwise(): weight * padded[:, k_row:k_row + strip_w, k_col:k_col + strip_h].astype(j...  2.93 us
  transfers between devices with their start and end apart: 19, of which 10 were waited for; matrix products, arithmetic and copies ran while one was open for 15% of the time, Pallas kernels for 0%

profile of v1, /device:TPU:3, one launch (start us, length us, event | category | flops | bytes accessed | tf_op | source)
XLA Modules:
  0.0 125.1 jit_solution(9274719811917397957)
XLA Ops:
  0.7 0.7 convert_bitcast_fusion
  1.5 1.0 bitcast_multiply_fusion.5
  2.6 4.1 %collective-permute-start = (bf16[96,3,128]{2,1,0:T(4,128)(2,1)S(1)}, bf16[96,3,128]{2,1,0:T(4,128)(2,1)S(1)}, u32[]{:S(2)}, u32[]{:S(2)}) collective-permute-start(bf16[96,3,128]{2,1,0:T(4,128)(2,1)S(1)} %get-tuple-element.82), channel_id=1, source_target_pairs={{0,4},{4,8},{8,12},{12,16},{16,20},{20,24},{24,28},{28,32},{32,36}... | collective-permute-start | bytes 221192 | tf_op jit(solution)/shard_map/ppermute | solution.py:25
  6.8 1.9 %collective-permute-start.1 = (bf16[96,3,128]{2,1,0:T(4,128)(2,1)S(1)}, bf16[96,3,128]{2,1,0:T(4,128)(2,1)S(1)}, u32[]{:S(2)}, u32[]{:S(2)}) collective-permute-start(bf16[96,3,128]{2,1,0:T(4,128)(2,1)S(1)} %get-tuple-element.83), channel_id=1, source_target_pairs={{4,0},{8,4},{12,8},{16,12},{20,16},{24,20},{28,24},{32,28},{36,32}... | collective-permute-start | bytes 221192 | tf_op jit(solution)/shard_map/ppermute | solution.py:28
  8.7 1.0 slice_bitcast_fusion.48
  9.7 1.0 slice_bitcast_fusion.47
  10.7 0.9 slice_bitcast_fusion.46
  11.7 1.2 fusion.19
  12.9 0.8 convert_reduce_fusion.3
  13.7 1.0 select_maximum_fusion.2
  14.8 11.6 %fusion.171 = (f32[16,128]{1,0:T(8,128)S(1)}, f32[96,16,128]{2,1,0:T(8,128)S(1)}) fusion(f32[96]{0:T(128)S(1)} %copy-done.7, bf16[96,22,134]{2,1,0:T(8,128)(2,1)S(1)} %select_maximum_fusion.2, f32[96]{0:T(128)S(1)} %get-tuple-element.134, f32[96]{0:T(128)S(1)} %get-tuple-element.135, f32[96]{0:T(128)S(1)} %get-tuple-element.88, ...), kind=kLoop, calls=%fused_computation.409 | loop fusion | flops 32634880 | bytes 17869568 | tf_op jit(solution)/shard_map/reduce_sum | solution.py:185
  26.9 1.0 fusion.7
  27.8 1.6 %fusion.5 = bf16[384,2048]{0,1:T(8,128)(2,1)S(1)} fusion(f32[2048,384]{1,0:T(8,128)S(1)} %get-tuple-element.137, bf16[96,384]{1,0:T(8,128)(2,1)S(1)} %copy-done.3, bf16[12,8,16,128]{3,2,1,0:T(8,128)(2,1)S(1)} %bitcast.266), kind=kOutput, calls=%fused_computation.59 | convolution fusion | flops 158859264 | bytes 5185536 | tf_op jit(solution)/shard_map/cf,cp->fp/dot_general | solution.py:148
  30.9 1.2 fusion.73
  32.6 7.6 %fusion.149 = (f32[96]{0:T(128)S(1)}, f32[96]{0:T(128)S(1)}, f32[96]{0:T(128)S(1)}, f32[96]{0:T(128)S(1)}, f32[96]{0:T(128)S(1)}, /*index=5*/f32[96]{0:T(128)S(1...) fusion(bf16[96,16,128]{2,1,0:T(8,128)(2,1)S(1)} %fusion.23, ...), kind=kLoop, calls=%fused_computation.270 | loop fusion | flops 10811712 | bytes 7478016 | tf_op jit(solution)/shard_map/reduce_sum | solution.py:125
  40.2 7.6 %fusion.150 = (f32[96]{0:T(128)S(1)}, f32[96]{0:T(128)S(1)}, f32[96]{0:T(128)S(1)}, f32[96]{0:T(128)S(1)}, f32[96]{0:T(128)S(1)}, /*index=5*/f32[96]{0:T(128)S(1...) fusion(bf16[96,16,128]{2,1,0:T(8,128)(2,1)S(1)} %fusion.23, ...), kind=kLoop, calls=%fused_computation.271 | loop fusion | flops 10811712 | bytes 7478016 | tf_op jit(solution)/shard_map/reduce_sum | solution.py:125
  47.8 2.1 %fusion.148 = (f32[96]{0:T(128)S(1)}, f32[96]{0:T(128)S(1)}, f32[96]{0:T(128)S(1)}, f32[96]{0:T(128)S(1)}, f32[96]{0:T(128)S(1)}, /*index=5*/f32[96]{0:T(128)S(1)}) fusion(bf16[96,16,128]{2,1,0:T(8,128)(2,1)S(1)} %fusion.23, bf16[96,22,134]{2,1,0:T(8,128)(2,1)S(1)} %select_maximum_fusion.2), kind=kLoop, calls=%fused_computation.269 | loop fusion | flops 3734976 | bytes 2754816 | tf_op jit(solution)/shard_map/reduce_sum | solution.py:125
  51.1 2.3 %fusion.147 = (f32[96]{0:T(128)S(1)}, f32[96]{0:T(128)S(1)}, f32[96]{0:T(128)S(1)}, f32[96]{0:T(128)S(1)}, f32[96]{0:T(128)S(1)}, /*index=5*/f32[96]{0:T(128)S(1)}, f32[96]{0:T(128)S(1)}, f32[96]{0:T(128)S(1)}) fusion(bf16[96,16,128]{2,1,0:T(8,128)(2,1)S(1)} %fusion.23, bf16[96,3,128]{2,1,0:T(4,128)(2,1)S(1)} %collective-permute-done.1, ...), kind=kLoop, calls=%fused_computation.268 | loop fusion | flops 8060160 | bytes 936960 | tf_op jit(solution)/shard_map/reduce_sum | solution.py:125
  54.0 1.4 %concatenate.35 = f32[79296]{0:T(1024)S(1)} concatenate(f32[73728]{0:T(1024)S(1)} %mul.1410, f32[4704]{0:T(1024)S(1)} %mul.1462, f32[480]{0:T(512)S(1)} %mul.1468, f32[384]{0:T(512)S(1)} %broadcast_multiply_fusion.4), dimensions={0} | concatenate | bytes 634368 | tf_op jit(solution)/shard_map/concatenate | solution.py:53
  55.5 1.8 %collective-permute-start.4 = (f32[160,128]{1,0:T(8,128)S(1)}, f32[160,128]{1,0:T(8,128)S(1)}, u32[]{:S(2)}, u32[]{:S(2)}) collective-permute-start(f32[160,128]{1,0:T(8,128)S(1)} %get-tuple-element.84), channel_id=1, source_target_pairs={{0,4},{4,8},{8,12},{12,0},{16,20},{20,24},{24,28},{28,16},{32,36},... | collective-permute-start | bytes 245768 | tf_op jit(solution)/shard_map/ppermute | solution.py:38
  57.3 3.4 %collective-permute-start.5 = (f32[160,128]{1,0:T(8,128)S(1)}, f32[160,128]{1,0:T(8,128)S(1)}, u32[]{:S(2)}, u32[]{:S(2)}) collective-permute-start(f32[160,128]{1,0:T(8,128)S(1)} %get-tuple-element.86), channel_id=1, source_target_pairs={{0,8},{4,12},{8,0},{12,4},{16,24},{20,28},{24,16},{28,20},{32,40},... | collective-permute-start | bytes 245768 | tf_op jit(solution)/shard_map/ppermute | solution.py:38
  60.7 3.8 %collective-permute-done.5 = f32[160,128]{1,0:T(8,128)S(1)} collective-permute-done((f32[160,128]{1,0:T(8,128)S(1)}, f32[160,128]{1,0:T(8,128)S(1)}, u32[]{:S(2)}, u32[]{:S(2)}) %collective-permute-start.5) | collective-permute-done | bytes 81952 | tf_op jit(solution)/shard_map/ppermute | solution.py:38
  64.4 0.7 collective-permute-done.6
  65.2 1.0 collective-permute-start.7
  66.3 2.6 %collective-permute-start.2 = (bf16[96,3,128]{2,1,0:T(4,128)(2,1)S(1)}, bf16[96,3,128]{2,1,0:T(4,128)(2,1)S(1)}, u32[]{:S(2)}, u32[]{:S(2)}) collective-permute-start(bf16[96,3,128]{2,1,0:T(4,128)(2,1)S(1)} %get-tuple-element.80), channel_id=1, source_target_pairs={{0,4},{4,8},{8,12},{12,16},{16,20},{20,24},{24,28},{28,32},{32,36}... | collective-permute-start | bytes 221192 | tf_op jit(solution)/shard_map/ppermute | solution.py:25
  68.9 1.9 %collective-permute-start.3 = (bf16[96,3,128]{2,1,0:T(4,128)(2,1)S(1)}, bf16[96,3,128]{2,1,0:T(4,128)(2,1)S(1)}, u32[]{:S(2)}, u32[]{:S(2)}) collective-permute-start(bf16[96,3,128]{2,1,0:T(4,128)(2,1)S(1)} %get-tuple-element.81), channel_id=1, source_target_pairs={{4,0},{8,4},{12,8},{16,12},{20,16},{24,20},{28,24},{32,28},{36,32}... | collective-permute-start | bytes 221192 | tf_op jit(solution)/shard_map/ppermute | solution.py:28
  70.8 3.6 %collective-permute-start.8 = (f32[160,128]{1,0:T(8,128)S(1)}, f32[160,128]{1,0:T(8,128)S(1)}, u32[]{:S(2)}, u32[]{:S(2)}) collective-permute-start(f32[160,128]{1,0:T(8,128)S(1)} %get-tuple-element.77), channel_id=1, source_target_pairs={{0,32},{4,36},{8,40},{12,44},{16,48},{20,52},{24,56},{28,60},{32,0... | collective-permute-start | bytes 245768 | tf_op jit(solution)/shard_map/ppermute | solution.py:38
  74.4 3.6 %collective-permute-start.9 = (f32[160,128]{1,0:T(8,128)S(1)}, f32[160,128]{1,0:T(8,128)S(1)}, u32[]{:S(2)}, u32[]{:S(2)}) collective-permute-start(f32[160,128]{1,0:T(8,128)S(1)} %get-tuple-element.77), channel_id=1, source_target_pairs={{0,48},{4,52},{8,56},{12,60},{16,0},{20,4},{24,8},{28,12},{32,16},... | collective-permute-start | bytes 245768 | tf_op jit(solution)/shard_map/ppermute | solution.py:38
  78.1 6.8 %collective-permute-done.9 = f32[160,128]{1,0:T(8,128)S(1)} collective-permute-done((f32[160,128]{1,0:T(8,128)S(1)}, f32[160,128]{1,0:T(8,128)S(1)}, u32[]{:S(2)}, u32[]{:S(2)}) %collective-permute-start.9) | collective-permute-done | bytes 81952 | tf_op jit(solution)/shard_map/ppermute | solution.py:38
  85.0 1.1 collective-permute-start.10
  86.2 1.0 multiply_convert_fusion
  87.2 0.8 collective-permute-start.11
  88.0 1.2 collective-permute-start.12
  89.2 2.9 %collective-permute-done.11 = f32[160,128]{1,0:T(8,128)S(1)} collective-permute-done((f32[160,128]{1,0:T(8,128)S(1)}, f32[160,128]{1,0:T(8,128)S(1)}, u32[]{:S(2)}, u32[]{:S(2)}) %collective-permute-start.11) | collective-permute-done | bytes 81952 | tf_op jit(solution)/shard_map/ppermute | solution.py:38
  92.2 1.4 %collective-permute-start.13 = (f32[160,128]{1,0:T(8,128)S(1)}, f32[160,128]{1,0:T(8,128)S(1)}, u32[]{:S(2)}, u32[]{:S(2)}) collective-permute-start(f32[160,128]{1,0:T(8,128)S(1)} %bitcast.276), channel_id=1, source_target_pairs={{0,1},{1,2},{2,3},{3,0},{4,5},{5,6},{6,7},{7,4},{8,9},{9,10},{10,1... | collective-permute-start | bytes 245768 | tf_op jit(solution)/shard_map/ppermute | solution.py:38
  93.6 1.0 select_maximum_fusion
  94.6 2.7 %collective-permute-start.14 = (f32[160,128]{1,0:T(8,128)S(1)}, f32[160,128]{1,0:T(8,128)S(1)}, u32[]{:S(2)}, u32[]{:S(2)}) collective-permute-start(f32[160,128]{1,0:T(8,128)S(1)} %bitcast.277), channel_id=1, source_target_pairs={{0,2},{1,3},{2,0},{3,1},{4,6},{5,7},{6,4},{7,5},{8,10},{9,11},{10,... | collective-permute-start | bytes 245768 | tf_op jit(solution)/shard_map/ppermute | solution.py:38
  97.4 1.1 collective-permute-start.15
  98.4 1.2 collective-permute-done.14
  99.6 1.1 collective-permute-done.15
  100.8 3.4 %collective-permute-start.16 = (f32[160,128]{1,0:T(8,128)S(1)}, f32[160,128]{1,0:T(8,128)S(1)}, u32[]{:S(2)}, u32[]{:S(2)}) collective-permute-start(f32[160,128]{1,0:T(8,128)S(1)} %get-tuple-element.71), channel_id=1, source_target_pairs={{0,4},{4,8},{8,12},{12,0},{16,20},{20,24},{24,28},{28,16},{32,36},... | collective-permute-start | bytes 245768 | tf_op jit(solution)/shard_map/ppermute | solution.py:38
  104.2 11.8 %fusion.164 = bf16[1,96,16,128]{3,2,1,0:T(8,128)(2,1)} fusion(bf16[96,22,134]{2,1,0:T(8,128)(2,1)S(1)} %select_maximum_fusion, f32[96]{0:T(128)S(1)} %get-tuple-element.87, f32[96]{0:T(128)S(1)} %get-tuple-element.106, f32[96]{0:T(128)S(1)} %get-tuple-element.125, bf16[96,3,128]{2,1,0:T(4,128)(2,1)S(1)} %collective-permute-done.3, ...), kind=kLoop, calls=%fused_computation.314 | loop fusion | flops 33030144 | bytes 17861504 | tf_op jit(solution)/shard_map/broadcast_in_dim | solution.py:231
  116.0 2.2 %collective-permute-start.17 = (f32[160,128]{1,0:T(8,128)S(1)}, f32[160,128]{1,0:T(8,128)S(1)}, u32[]{:S(2)}, u32[]{:S(2)}) collective-permute-start(f32[160,128]{1,0:T(8,128)S(1)} %get-tuple-element.71), channel_id=1, source_target_pairs={{0,8},{4,12},{8,0},{12,4},{16,24},{20,28},{24,16},{28,20},{32,40},... | collective-permute-start | bytes 245768 | tf_op jit(solution)/shard_map/ppermute | solution.py:38
  118.2 2.2 %collective-permute-done.17 = f32[160,128]{1,0:T(8,128)S(1)} collective-permute-done((f32[160,128]{1,0:T(8,128)S(1)}, f32[160,128]{1,0:T(8,128)S(1)}, u32[]{:S(2)}, u32[]{:S(2)}) %collective-permute-start.17) | collective-permute-done | bytes 81952 | tf_op jit(solution)/shard_map/ppermute | solution.py:38
  120.4 1.6 %collective-permute-done.18 = f32[160,128]{1,0:T(8,128)S(1)} collective-permute-done((f32[160,128]{1,0:T(8,128)S(1)}, f32[160,128]{1,0:T(8,128)S(1)}, u32[]{:S(2)}, u32[]{:S(2)}) %collective-permute-start.18) | collective-permute-done | bytes 81952 | tf_op jit(solution)/shard_map/ppermute | solution.py:38
  122.8 0.8 reshape.231
  123.7 0.7 copy.19
  124.4 0.7 reshape.234
  (91 shorter events, 5.9 us)
Async XLA Ops:
  0.6 26.2 %copy-start = (bf16[96,384]{1,0:T(8,128)(2,1)S(1)}, bf16[96,384]{1,0:T(8,128)(2,1)}, u32[]{:S(2)}) copy-start(bf16[96,384]{1,0:T(8,128)(2,1)} %param.19) | copy-start | bytes 221188
  0.6 14.1 %copy-start.7 = (f32[96]{0:T(128)S(1)}, f32[96]{0:T(128)}, u32[]{:S(2)}) copy-start(f32[96]{0:T(128)} %param.16) | copy-start | bytes 1156
  2.6 11.1 %collective-permute-start = (bf16[96,3,128]{2,1,0:T(4,128)(2,1)S(1)}, bf16[96,3,128]{2,1,0:T(4,128)(2,1)S(1)}, u32[]{:S(2)}, u32[]{:S(2)}) collective-permute-start(bf16[96,3,128]{2,1,0:T(4,128)(2,1)S(1)} %get-tuple-element.82), channel_id=1, source_target_pairs={{0,4},{4,8},{8,12},{12,16},{16,20},{20,24},{24,28},{28,32},{32,36}... | collective-permute-start | bytes 221192 | tf_op jit(solution)/shard_map/ppermute | solution.py:25
  6.8 7.0 %collective-permute-start.1 = (bf16[96,3,128]{2,1,0:T(4,128)(2,1)S(1)}, bf16[96,3,128]{2,1,0:T(4,128)(2,1)S(1)}, u32[]{:S(2)}, u32[]{:S(2)}) collective-permute-start(bf16[96,3,128]{2,1,0:T(4,128)(2,1)S(1)} %get-tuple-element.83), channel_id=1, source_target_pairs={{4,0},{8,4},{12,8},{16,12},{20,16},{24,20},{28,24},{32,28},{36,32}... | collective-permute-start | bytes 221192 | tf_op jit(solution)/shard_map/ppermute | solution.py:28
  14.8 11.8 %copy-start.4 = (f32[96]{0:T(128)S(1)}, f32[96]{0:T(128)}, u32[]{:S(2)}) copy-start(f32[96]{0:T(128)} %param.17) | copy-start | bytes 1156
  14.8 11.7 %copy-start.8 = (f32[96]{0:T(128)S(1)}, f32[96]{0:T(128)}, u32[]{:S(2)}) copy-start(f32[96]{0:T(128)} %param.18) | copy-start | bytes 1156
  14.8 12.0 %copy-start.6 = (f32[384]{0:T(512)S(1)}, f32[384]{0:T(512)}, u32[]{:S(2)}) copy-start(f32[384]{0:T(512)} %param.20) | copy-start | bytes 4612
  26.8 1.0 copy-start.3
  29.5 0.7 copy-start.9
  29.5 1.4 %copy-start.1 = (bf16[1,96,16,128]{3,2,1,0:T(8,128)(2,1)S(1)}, bf16[1,96,16,128]{3,2,1,0:T(8,128)(2,1)}, u32[]{:S(2)}) copy-start(bf16[1,96,16,128]{3,2,1,0:T(8,128)(2,1)} %param.13) | copy-start | bytes 1179652
  54.0 32.1 %copy-start.2 = (bf16[1,96,16,128]{3,2,1,0:T(8,128)(2,1)S(1)}, bf16[1,96,16,128]{3,2,1,0:T(8,128)(2,1)}, u32[]{:S(2)}) copy-start(bf16[1,96,16,128]{3,2,1,0:T(8,128)(2,1)} %param.12) | copy-start | bytes 1179652
  54.0 32.1 %copy-start.5 = (f32[96]{0:T(128)S(1)}, f32[96]{0:T(128)}, u32[]{:S(2)}) copy-start(f32[96]{0:T(128)} %param.23) | copy-start | bytes 1156
  55.5 5.2 %collective-permute-start.4 = (f32[160,128]{1,0:T(8,128)S(1)}, f32[160,128]{1,0:T(8,128)S(1)}, u32[]{:S(2)}, u32[]{:S(2)}) collective-permute-start(f32[160,128]{1,0:T(8,128)S(1)} %get-tuple-element.84), channel_id=1, source_target_pairs={{0,4},{4,8},{8,12},{12,0},{16,20},{20,24},{24,28},{28,16},{32,36},... | collective-permute-start | bytes 245768 | tf_op jit(solution)/shard_map/ppermute | solution.py:38
  57.3 7.1 %collective-permute-start.5 = (f32[160,128]{1,0:T(8,128)S(1)}, f32[160,128]{1,0:T(8,128)S(1)}, u32[]{:S(2)}, u32[]{:S(2)}) collective-permute-start(f32[160,128]{1,0:T(8,128)S(1)} %get-tuple-element.86), channel_id=1, source_target_pairs={{0,8},{4,12},{8,0},{12,4},{16,24},{20,28},{24,16},{28,20},{32,40},... | collective-permute-start | bytes 245768 | tf_op jit(solution)/shard_map/ppermute | solution.py:38
  60.7 4.5 %collective-permute-start.6 = (f32[160,128]{1,0:T(8,128)S(1)}, f32[160,128]{1,0:T(8,128)S(1)}, u32[]{:S(2)}, u32[]{:S(2)}) collective-permute-start(f32[160,128]{1,0:T(8,128)S(1)} %get-tuple-element.85), channel_id=1, source_target_pairs={{0,12},{4,0},{8,4},{12,8},{16,28},{20,16},{24,20},{28,24},{32,44},... | collective-permute-start | bytes 245768 | tf_op jit(solution)/shard_map/ppermute | solution.py:38
  65.2 12.8 %collective-permute-start.7 = (f32[160,128]{1,0:T(8,128)S(1)}, f32[160,128]{1,0:T(8,128)S(1)}, u32[]{:S(2)}, u32[]{:S(2)}) collective-permute-start(f32[160,128]{1,0:T(8,128)S(1)} %get-tuple-element.77), channel_id=1, source_target_pairs={{0,16},{4,20},{8,24},{12,28},{16,32},{20,36},{24,40},{28,44},{32,4... | collective-permute-start | bytes 245768 | tf_op jit(solution)/shard_map/ppermute | solution.py:38
  66.3 27.3 %collective-permute-start.2 = (bf16[96,3,128]{2,1,0:T(4,128)(2,1)S(1)}, bf16[96,3,128]{2,1,0:T(4,128)(2,1)S(1)}, u32[]{:S(2)}, u32[]{:S(2)}) collective-permute-start(bf16[96,3,128]{2,1,0:T(4,128)(2,1)S(1)} %get-tuple-element.80), channel_id=1, source_target_pairs={{0,4},{4,8},{8,12},{12,16},{16,20},{20,24},{24,28},{28,32},{32,36}... | collective-permute-start | bytes 221192 | tf_op jit(solution)/shard_map/ppermute | solution.py:25
  68.9 24.7 %collective-permute-start.3 = (bf16[96,3,128]{2,1,0:T(4,128)(2,1)S(1)}, bf16[96,3,128]{2,1,0:T(4,128)(2,1)S(1)}, u32[]{:S(2)}, u32[]{:S(2)}) collective-permute-start(bf16[96,3,128]{2,1,0:T(4,128)(2,1)S(1)} %get-tuple-element.81), channel_id=1, source_target_pairs={{4,0},{8,4},{12,8},{16,12},{20,16},{24,20},{28,24},{32,28},{36,32}... | collective-permute-start | bytes 221192 | tf_op jit(solution)/shard_map/ppermute | solution.py:28
  70.8 7.3 %collective-permute-start.8 = (f32[160,128]{1,0:T(8,128)S(1)}, f32[160,128]{1,0:T(8,128)S(1)}, u32[]{:S(2)}, u32[]{:S(2)}) collective-permute-start(f32[160,128]{1,0:T(8,128)S(1)} %get-tuple-element.77), channel_id=1, source_target_pairs={{0,32},{4,36},{8,40},{12,44},{16,48},{20,52},{24,56},{28,60},{32,0... | collective-permute-start | bytes 245768 | tf_op jit(solution)/shard_map/ppermute | solution.py:38
  74.4 10.5 %collective-permute-start.9 = (f32[160,128]{1,0:T(8,128)S(1)}, f32[160,128]{1,0:T(8,128)S(1)}, u32[]{:S(2)}, u32[]{:S(2)}) collective-permute-start(f32[160,128]{1,0:T(8,128)S(1)} %get-tuple-element.77), channel_id=1, source_target_pairs={{0,48},{4,52},{8,56},{12,60},{16,0},{20,4},{24,8},{28,12},{32,16},... | collective-permute-start | bytes 245768 | tf_op jit(solution)/shard_map/ppermute | solution.py:38
  85.0 4.2 %collective-permute-start.10 = (f32[160,128]{1,0:T(8,128)S(1)}, f32[160,128]{1,0:T(8,128)S(1)}, u32[]{:S(2)}, u32[]{:S(2)}) collective-permute-start(f32[160,128]{1,0:T(8,128)S(1)} %bitcast.279), channel_id=1, source_target_pairs={{0,64},{4,68},{8,72},{12,76},{16,80},{20,84},{24,88},{28,92},{32,9... | collective-permute-start | bytes 245768 | tf_op jit(solution)/shard_map/ppermute | solution.py:38
  87.2 4.9 %collective-permute-start.11 = (f32[160,128]{1,0:T(8,128)S(1)}, f32[160,128]{1,0:T(8,128)S(1)}, u32[]{:S(2)}, u32[]{:S(2)}) collective-permute-start(f32[160,128]{1,0:T(8,128)S(1)} %bitcast.280), channel_id=1, source_target_pairs={{0,128},{4,132},{8,136},{12,140},{16,144},{20,148},{24,152},{28,15... | collective-permute-start | bytes 245768 | tf_op jit(solution)/shard_map/ppermute | solution.py:38
  88.0 4.2 %collective-permute-start.12 = (f32[160,128]{1,0:T(8,128)S(1)}, f32[160,128]{1,0:T(8,128)S(1)}, u32[]{:S(2)}, u32[]{:S(2)}) collective-permute-start(f32[160,128]{1,0:T(8,128)S(1)} %bitcast.281), channel_id=1, source_target_pairs={{0,192},{4,196},{8,200},{12,204},{16,208},{20,212},{24,216},{28,22... | collective-permute-start | bytes 245768 | tf_op jit(solution)/shard_map/ppermute | solution.py:38
  92.2 6.2 %collective-permute-start.13 = (f32[160,128]{1,0:T(8,128)S(1)}, f32[160,128]{1,0:T(8,128)S(1)}, u32[]{:S(2)}, u32[]{:S(2)}) collective-permute-start(f32[160,128]{1,0:T(8,128)S(1)} %bitcast.276), channel_id=1, source_target_pairs={{0,1},{1,2},{2,3},{3,0},{4,5},{5,6},{6,7},{7,4},{8,9},{9,10},{10,1... | collective-permute-start | bytes 245768 | tf_op jit(solution)/shard_map/ppermute | solution.py:38
  94.6 4.9 %collective-permute-start.14 = (f32[160,128]{1,0:T(8,128)S(1)}, f32[160,128]{1,0:T(8,128)S(1)}, u32[]{:S(2)}, u32[]{:S(2)}) collective-permute-start(f32[160,128]{1,0:T(8,128)S(1)} %bitcast.277), channel_id=1, source_target_pairs={{0,2},{1,3},{2,0},{3,1},{4,6},{5,7},{6,4},{7,5},{8,10},{9,11},{10,... | collective-permute-start | bytes 245768 | tf_op jit(solution)/shard_map/ppermute | solution.py:38
  97.4 3.3 %collective-permute-start.15 = (f32[160,128]{1,0:T(8,128)S(1)}, f32[160,128]{1,0:T(8,128)S(1)}, u32[]{:S(2)}, u32[]{:S(2)}) collective-permute-start(f32[160,128]{1,0:T(8,128)S(1)} %bitcast.278), channel_id=1, source_target_pairs={{0,3},{1,0},{2,1},{3,2},{4,7},{5,4},{6,5},{7,6},{8,11},{9,8},{10,9... | collective-permute-start | bytes 245768 | tf_op jit(solution)/shard_map/ppermute | solution.py:38
  100.8 17.4 %collective-permute-start.16 = (f32[160,128]{1,0:T(8,128)S(1)}, f32[160,128]{1,0:T(8,128)S(1)}, u32[]{:S(2)}, u32[]{:S(2)}) collective-permute-start(f32[160,128]{1,0:T(8,128)S(1)} %get-tuple-element.71), channel_id=1, source_target_pairs={{0,4},{4,8},{8,12},{12,0},{16,20},{20,24},{24,28},{28,16},{32,36},... | collective-permute-start | bytes 245768 | tf_op jit(solution)/shard_map/ppermute | solution.py:38
  116.0 4.4 %collective-permute-start.17 = (f32[160,128]{1,0:T(8,128)S(1)}, f32[160,128]{1,0:T(8,128)S(1)}, u32[]{:S(2)}, u32[]{:S(2)}) collective-permute-start(f32[160,128]{1,0:T(8,128)S(1)} %get-tuple-element.71), channel_id=1, source_target_pairs={{0,8},{4,12},{8,0},{12,4},{16,24},{20,28},{24,16},{28,20},{32,40},... | collective-permute-start | bytes 245768 | tf_op jit(solution)/shard_map/ppermute | solution.py:38
  118.1 3.9 %collective-permute-start.18 = (f32[160,128]{1,0:T(8,128)S(1)}, f32[160,128]{1,0:T(8,128)S(1)}, u32[]{:S(2)}, u32[]{:S(2)}) collective-permute-start(f32[160,128]{1,0:T(8,128)S(1)} %get-tuple-element.71), channel_id=1, source_target_pairs={{0,12},{4,0},{8,4},{12,8},{16,28},{20,16},{24,20},{28,24},{32,44},... | collective-permute-start | bytes 245768 | tf_op jit(solution)/shard_map/ppermute | solution.py:38

commit v2 on v1

--- a/solution.py
+++ b/solution.py
@@ -49,7 +49,7 @@
     return groups
 
 
-def summed_everywhere(parts, axes, lanes=128, halvings=1):
+def summed_everywhere(parts, axes, lanes=128, halvings=0):
     flat = jnp.concatenate([p.reshape(-1) for p in parts])
     rows = -(-flat.shape[0] // lanes)
     rows += (-rows) % 128

time: 126 us -> 160 us (1.27)
  waiting for transfers between devices: 20.4 us -> 58.3 us
  starting transfers between devices: 37.8 us -> 33 us
    ppermute x15 -> x12, waiting for transfers between devices: 20.4 us -> 58.2 us  [shifted(): return lax.ppermute(values, axis, pairs)]
    ppermute x15 -> x12, starting transfers between devices: 27.2 us -> 22.6 us  [shifted(): return lax.ppermute(values, axis, pairs)]
  transfers between devices with their start and end apart: 19 -> 16, of which waited for: 10 -> 11; matrix products, arithmetic and copies ran while one was open for 15% -> 12% of each run, Pallas kernels for 0% -> 0%
where the time goes in v2:
time: 160 us; the launch traced here: 159 us
  waiting for transfers between devices  58.3 us (36%)
  other arithmetic  52.2 us (33%)
  starting transfers between devices  33 us (21%)
  local copies, waits for them, and re-layouts  9.37 us (6%)
  matrix products  4.65 us (3%)
    ppermute x12, waiting for transfers between devices, shifted(): return lax.ppermute(values, axis, pairs)  58.2 us
    ppermute x12, starting transfers between devices, shifted(): return lax.ppermute(values, axis, pairs)  22.6 us
    reduce_sum x4, other arithmetic, kernel_sums(): entries.append(jnp.sum(grad_f * piece, axis=(1, 2)))  19.6 us
    broadcast_in_dim x1, other arithmetic, on_device(): grad_image[None]  11.8 us
    reduce_sum x1, other arithmetic, on_device(): centered = pre - jnp.mean(pre, axis=0, keepdims=True)  11.6 us
    ppermute x2, starting transfers between devices, extended(): lax.ppermute(lax.slice_in_dim(block, block.shape[dim] - width, None, axis...  6.13 us
    ppermute x2, starting transfers between devices, extended(): lax.ppermute(lax.slice_in_dim(block, 0, width, axis=dim), axis, backward)  4.22 us
  transfers between devices with their start and end apart: 16, of which 11 were waited for; matrix products, arithmetic and copies ran while one was open for 12% of the time, Pallas kernels for 0%

profile of v2, /device:TPU:3, one launch (start us, length us, event | category | flops | bytes accessed | tf_op | source)
XLA Modules:
  0.0 158.6 jit_solution(7087056829303331176)
XLA Ops:
  0.7 0.7 convert_bitcast_fusion
  1.5 1.0 bitcast_multiply_fusion.5
  2.7 4.1 %collective-permute-start = (bf16[96,3,128]{2,1,0:T(4,128)(2,1)S(1)}, bf16[96,3,128]{2,1,0:T(4,128)(2,1)S(1)}, u32[]{:S(2)}, u32[]{:S(2)}) collective-permute-start(bf16[96,3,128]{2,1,0:T(4,128)(2,1)S(1)} %get-tuple-element.80), channel_id=1, source_target_pairs={{0,4},{4,8},{8,12},{12,16},{16,20},{20,24},{24,28},{28,32},{32,36}... | collective-permute-start | bytes 221192 | tf_op jit(solution)/shard_map/ppermute | solution.py:25
  6.8 1.9 %collective-permute-start.1 = (bf16[96,3,128]{2,1,0:T(4,128)(2,1)S(1)}, bf16[96,3,128]{2,1,0:T(4,128)(2,1)S(1)}, u32[]{:S(2)}, u32[]{:S(2)}) collective-permute-start(bf16[96,3,128]{2,1,0:T(4,128)(2,1)S(1)} %get-tuple-element.81), channel_id=1, source_target_pairs={{4,0},{8,4},{12,8},{16,12},{20,16},{24,20},{28,24},{32,28},{36,32}... | collective-permute-start | bytes 221192 | tf_op jit(solution)/shard_map/ppermute | solution.py:28
  8.7 1.0 slice_bitcast_fusion.48
  9.7 1.0 slice_bitcast_fusion.47
  10.7 0.9 slice_bitcast_fusion.46
  11.7 0.8 fusion.19
  12.5 0.8 convert_reduce_fusion.3
  13.3 1.0 select_maximum_fusion.2
  14.4 11.6 %fusion.169 = (f32[16,128]{1,0:T(8,128)S(1)}, f32[96,16,128]{2,1,0:T(8,128)S(1)}) fusion(f32[96]{0:T(128)S(1)} %copy-done.7, bf16[96,22,134]{2,1,0:T(8,128)(2,1)S(1)} %select_maximum_fusion.2, f32[96]{0:T(128)S(1)} %get-tuple-element.129, f32[96]{0:T(128)S(1)} %get-tuple-element.130, f32[96]{0:T(128)S(1)} %get-tuple-element.83, ...), kind=kLoop, calls=%fused_computation.407 | loop fusion | flops 32634880 | bytes 17869568 | tf_op jit(solution)/shard_map/reduce_sum | solution.py:185
  26.6 1.0 fusion.7
  27.6 1.6 %fusion.5 = bf16[384,2048]{0,1:T(8,128)(2,1)S(1)} fusion(f32[2048,384]{1,0:T(8,128)S(1)} %get-tuple-element.132, bf16[96,384]{1,0:T(8,128)(2,1)S(1)} %copy-done.3, bf16[12,8,16,128]{3,2,1,0:T(8,128)(2,1)S(1)} %bitcast.271), kind=kOutput, calls=%fused_computation.59 | convolution fusion | flops 158859264 | bytes 5185536 | tf_op jit(solution)/shard_map/cf,cp->fp/dot_general | solution.py:148
  30.7 1.2 fusion.73
  32.4 7.6 %fusion.149 = (f32[96]{0:T(128)S(1)}, f32[96]{0:T(128)S(1)}, f32[96]{0:T(128)S(1)}, f32[96]{0:T(128)S(1)}, f32[96]{0:T(128)S(1)}, /*index=5*/f32[96]{0:T(128)S(1...) fusion(bf16[96,16,128]{2,1,0:T(8,128)(2,1)S(1)} %fusion.23, ...), kind=kLoop, calls=%fused_computation.270 | loop fusion | flops 10811712 | bytes 7478016 | tf_op jit(solution)/shard_map/reduce_sum | solution.py:125
  40.0 7.6 %fusion.150 = (f32[96]{0:T(128)S(1)}, f32[96]{0:T(128)S(1)}, f32[96]{0:T(128)S(1)}, f32[96]{0:T(128)S(1)}, f32[96]{0:T(128)S(1)}, /*index=5*/f32[96]{0:T(128)S(1...) fusion(bf16[96,16,128]{2,1,0:T(8,128)(2,1)S(1)} %fusion.23, ...), kind=kLoop, calls=%fused_computation.271 | loop fusion | flops 10811712 | bytes 7478016 | tf_op jit(solution)/shard_map/reduce_sum | solution.py:125
  47.6 2.1 %fusion.148 = (f32[96]{0:T(128)S(1)}, f32[96]{0:T(128)S(1)}, f32[96]{0:T(128)S(1)}, f32[96]{0:T(128)S(1)}, f32[96]{0:T(128)S(1)}, /*index=5*/f32[96]{0:T(128)S(1)}) fusion(bf16[96,16,128]{2,1,0:T(8,128)(2,1)S(1)} %fusion.23, bf16[96,22,134]{2,1,0:T(8,128)(2,1)S(1)} %select_maximum_fusion.2), kind=kLoop, calls=%fused_computation.269 | loop fusion | flops 3734976 | bytes 2754816 | tf_op jit(solution)/shard_map/reduce_sum | solution.py:125
  50.8 2.3 %fusion.147 = (f32[96]{0:T(128)S(1)}, f32[96]{0:T(128)S(1)}, f32[96]{0:T(128)S(1)}, f32[96]{0:T(128)S(1)}, f32[96]{0:T(128)S(1)}, /*index=5*/f32[96]{0:T(128)S(1)}, f32[96]{0:T(128)S(1)}, f32[96]{0:T(128)S(1)}) fusion(bf16[96,16,128]{2,1,0:T(8,128)(2,1)S(1)} %fusion.23, bf16[96,3,128]{2,1,0:T(4,128)(2,1)S(1)} %collective-permute-done.1, ...), kind=kLoop, calls=%fused_computation.268 | loop fusion | flops 8060160 | bytes 936960 | tf_op jit(solution)/shard_map/reduce_sum | solution.py:125
  53.8 1.4 concatenate.35
  55.2 1.8 %collective-permute-start.4 = (f32[640,128]{1,0:T(8,128)S(1)}, f32[640,128]{1,0:T(8,128)S(1)}, u32[]{:S(2)}, u32[]{:S(2)}) collective-permute-start(f32[640,128]{1,0:T(8,128)S(1)} %pad_bitcast_fusion), channel_id=1, source_target_pairs={{0,4},{4,8},{8,12},{12,0},{16,20},{20,24},{24,28},{28,16},{32,36},... | collective-permute-start | bytes 983048 | tf_op jit(solution)/shard_map/ppermute | solution.py:38
  57.0 3.4 %collective-permute-start.5 = (f32[640,128]{1,0:T(8,128)S(1)}, f32[640,128]{1,0:T(8,128)S(1)}, u32[]{:S(2)}, u32[]{:S(2)}) collective-permute-start(f32[640,128]{1,0:T(8,128)S(1)} %pad_bitcast_fusion), channel_id=1, source_target_pairs={{0,8},{4,12},{8,0},{12,4},{16,24},{20,28},{24,16},{28,20},{32,40},... | collective-permute-start | bytes 983048 | tf_op jit(solution)/shard_map/ppermute | solution.py:38
  60.5 1.6 %collective-permute-done.4 = f32[640,128]{1,0:T(8,128)S(1)} collective-permute-done((f32[640,128]{1,0:T(8,128)S(1)}, f32[640,128]{1,0:T(8,128)S(1)}, u32[]{:S(2)}, u32[]{:S(2)}) %collective-permute-start.4) | collective-permute-done | bytes 327712 | tf_op jit(solution)/shard_map/ppermute | solution.py:38
  62.2 12.4 %collective-permute-done.5 = f32[640,128]{1,0:T(8,128)S(1)} collective-permute-done((f32[640,128]{1,0:T(8,128)S(1)}, f32[640,128]{1,0:T(8,128)S(1)}, u32[]{:S(2)}, u32[]{:S(2)}) %collective-permute-start.5) | collective-permute-done | bytes 327712 | tf_op jit(solution)/shard_map/ppermute | solution.py:38
  74.6 0.8 collective-permute-done.6
  75.6 1.4 collective-permute-start.7
  77.0 3.6 %collective-permute-start.8 = (f32[640,128]{1,0:T(8,128)S(1)}, f32[640,128]{1,0:T(8,128)S(1)}, u32[]{:S(2)}, u32[]{:S(2)}) collective-permute-start(f32[640,128]{1,0:T(8,128)S(1)} %bitcast.279), channel_id=1, source_target_pairs={{0,32},{4,36},{8,40},{12,44},{16,48},{20,52},{24,56},{28,60},{32,0... | collective-permute-start | bytes 983048 | tf_op jit(solution)/shard_map/ppermute | solution.py:38
  80.7 2.0 %collective-permute-start.2 = (bf16[96,3,128]{2,1,0:T(4,128)(2,1)S(1)}, bf16[96,3,128]{2,1,0:T(4,128)(2,1)S(1)}, u32[]{:S(2)}, u32[]{:S(2)}) collective-permute-start(bf16[96,3,128]{2,1,0:T(4,128)(2,1)S(1)} %get-tuple-element.78), channel_id=1, source_target_pairs={{0,4},{4,8},{8,12},{12,16},{16,20},{20,24},{24,28},{28,32},{32,36}... | collective-permute-start | bytes 221192 | tf_op jit(solution)/shard_map/ppermute | solution.py:25
  82.7 2.3 %collective-permute-start.3 = (bf16[96,3,128]{2,1,0:T(4,128)(2,1)S(1)}, bf16[96,3,128]{2,1,0:T(4,128)(2,1)S(1)}, u32[]{:S(2)}, u32[]{:S(2)}) collective-permute-start(bf16[96,3,128]{2,1,0:T(4,128)(2,1)S(1)} %get-tuple-element.79), channel_id=1, source_target_pairs={{4,0},{8,4},{12,8},{16,12},{20,16},{24,20},{28,24},{32,28},{36,32}... | collective-permute-start | bytes 221192 | tf_op jit(solution)/shard_map/ppermute | solution.py:28
  85.0 3.3 %collective-permute-start.9 = (f32[640,128]{1,0:T(8,128)S(1)}, f32[640,128]{1,0:T(8,128)S(1)}, u32[]{:S(2)}, u32[]{:S(2)}) collective-permute-start(f32[640,128]{1,0:T(8,128)S(1)} %bitcast.280), channel_id=1, source_target_pairs={{0,48},{4,52},{8,56},{12,60},{16,0},{20,4},{24,8},{28,12},{32,16},... | collective-permute-start | bytes 983048 | tf_op jit(solution)/shard_map/ppermute | solution.py:38
  88.3 0.8 collective-permute-done.7
  89.1 10.2 %collective-permute-done.8 = f32[640,128]{1,0:T(8,128)S(1)} collective-permute-done((f32[640,128]{1,0:T(8,128)S(1)}, f32[640,128]{1,0:T(8,128)S(1)}, u32[]{:S(2)}, u32[]{:S(2)}) %collective-permute-start.8) | collective-permute-done | bytes 327712 | tf_op jit(solution)/shard_map/ppermute | solution.py:38
  99.4 11.1 %collective-permute-done.9 = f32[640,128]{1,0:T(8,128)S(1)} collective-permute-done((f32[640,128]{1,0:T(8,128)S(1)}, f32[640,128]{1,0:T(8,128)S(1)}, u32[]{:S(2)}, u32[]{:S(2)}) %collective-permute-start.9) | collective-permute-done | bytes 327712 | tf_op jit(solution)/shard_map/ppermute | solution.py:38
  110.7 1.3 collective-permute-start.10
  112.0 1.0 multiply_convert_fusion
  113.0 1.5 collective-permute-start.11
  114.5 1.0 select_maximum_fusion
  115.5 1.3 collective-permute-start.12
  116.9 1.8 %collective-permute-done.10 = f32[640,128]{1,0:T(8,128)S(1)} collective-permute-done((f32[640,128]{1,0:T(8,128)S(1)}, f32[640,128]{1,0:T(8,128)S(1)}, u32[]{:S(2)}, u32[]{:S(2)}) %collective-permute-start.10) | collective-permute-done | bytes 327712 | tf_op jit(solution)/shard_map/ppermute | solution.py:38
  118.7 3.5 %collective-permute-done.11 = f32[640,128]{1,0:T(8,128)S(1)} collective-permute-done((f32[640,128]{1,0:T(8,128)S(1)}, f32[640,128]{1,0:T(8,128)S(1)}, u32[]{:S(2)}, u32[]{:S(2)}) %collective-permute-start.11) | collective-permute-done | bytes 327712 | tf_op jit(solution)/shard_map/ppermute | solution.py:38
  122.2 9.0 %collective-permute-done.12 = f32[640,128]{1,0:T(8,128)S(1)} collective-permute-done((f32[640,128]{1,0:T(8,128)S(1)}, f32[640,128]{1,0:T(8,128)S(1)}, u32[]{:S(2)}, u32[]{:S(2)}) %collective-permute-start.12) | collective-permute-done | bytes 327712 | tf_op jit(solution)/shard_map/ppermute | solution.py:38
  131.4 1.4 collective-permute-start.13
  132.7 2.6 %collective-permute-start.14 = (f32[640,128]{1,0:T(8,128)S(1)}, f32[640,128]{1,0:T(8,128)S(1)}, u32[]{:S(2)}, u32[]{:S(2)}) collective-permute-start(f32[640,128]{1,0:T(8,128)S(1)} %bitcast.282), channel_id=1, source_target_pairs={{0,2},{1,3},{2,0},{3,1},{4,6},{5,7},{6,4},{7,5},{8,10},{9,11},{10,... | collective-permute-start | bytes 983048 | tf_op jit(solution)/shard_map/ppermute | solution.py:38
  135.4 11.8 %fusion.164 = bf16[1,96,16,128]{3,2,1,0:T(8,128)(2,1)} fusion(bf16[96,22,134]{2,1,0:T(8,128)(2,1)S(1)} %select_maximum_fusion, f32[96]{0:T(128)S(1)} %get-tuple-element.82, f32[96]{0:T(128)S(1)} %get-tuple-element.101, f32[96]{0:T(128)S(1)} %get-tuple-element.120, bf16[96,3,128]{2,1,0:T(4,128)(2,1)S(1)} %collective-permute-done.3, ...), kind=kLoop, calls=%fused_computation.314 | loop fusion | flops 33030144 | bytes 17861504 | tf_op jit(solution)/shard_map/broadcast_in_dim | solution.py:231
  147.1 1.1 collective-permute-start.15
  148.2 1.5 collective-permute-done.14
  149.7 5.6 %collective-permute-done.15 = f32[640,128]{1,0:T(8,128)S(1)} collective-permute-done((f32[640,128]{1,0:T(8,128)S(1)}, f32[640,128]{1,0:T(8,128)S(1)}, u32[]{:S(2)}, u32[]{:S(2)}) %collective-permute-start.15) | collective-permute-done | bytes 327712 | tf_op jit(solution)/shard_map/ppermute | solution.py:38
  156.3 0.8 reshape.242
  157.2 0.7 copy.19
  (86 shorter events, 7.2 us)
Async XLA Ops:
  0.6 25.8 %copy-start = (bf16[96,384]{1,0:T(8,128)(2,1)S(1)}, bf16[96,384]{1,0:T(8,128)(2,1)}, u32[]{:S(2)}) copy-start(bf16[96,384]{1,0:T(8,128)(2,1)} %param.19) | copy-start | bytes 221188
  0.6 11.0 %copy-start.1 = (bf16[1,96,16,128]{3,2,1,0:T(8,128)(2,1)S(1)}, bf16[1,96,16,128]{3,2,1,0:T(8,128)(2,1)}, u32[]{:S(2)}) copy-start(bf16[1,96,16,128]{3,2,1,0:T(8,128)(2,1)} %param.13) | copy-start | bytes 1179652
  2.7 10.7 %collective-permute-start = (bf16[96,3,128]{2,1,0:T(4,128)(2,1)S(1)}, bf16[96,3,128]{2,1,0:T(4,128)(2,1)S(1)}, u32[]{:S(2)}, u32[]{:S(2)}) collective-permute-start(bf16[96,3,128]{2,1,0:T(4,128)(2,1)S(1)} %get-tuple-element.80), channel_id=1, source_target_pairs={{0,4},{4,8},{8,12},{12,16},{16,20},{20,24},{24,28},{28,32},{32,36}... | collective-permute-start | bytes 221192 | tf_op jit(solution)/shard_map/ppermute | solution.py:25
  6.8 6.5 %collective-permute-start.1 = (bf16[96,3,128]{2,1,0:T(4,128)(2,1)S(1)}, bf16[96,3,128]{2,1,0:T(4,128)(2,1)S(1)}, u32[]{:S(2)}, u32[]{:S(2)}) collective-permute-start(bf16[96,3,128]{2,1,0:T(4,128)(2,1)S(1)} %get-tuple-element.81), channel_id=1, source_target_pairs={{4,0},{8,4},{12,8},{16,12},{20,16},{24,20},{28,24},{32,28},{36,32}... | collective-permute-start | bytes 221192 | tf_op jit(solution)/shard_map/ppermute | solution.py:28
  12.5 1.9 %copy-start.7 = (f32[96]{0:T(128)S(1)}, f32[96]{0:T(128)}, u32[]{:S(2)}) copy-start(f32[96]{0:T(128)} %param.16) | copy-start | bytes 1156
  14.4 11.8 %copy-start.4 = (f32[96]{0:T(128)S(1)}, f32[96]{0:T(128)}, u32[]{:S(2)}) copy-start(f32[96]{0:T(128)} %param.17) | copy-start | bytes 1156
  14.4 11.7 %copy-start.8 = (f32[96]{0:T(128)S(1)}, f32[96]{0:T(128)}, u32[]{:S(2)}) copy-start(f32[96]{0:T(128)} %param.18) | copy-start | bytes 1156
  26.0 0.7 copy-start.6
  26.6 1.0 copy-start.3
  29.3 0.7 copy-start.9
  55.2 6.9 %collective-permute-start.4 = (f32[640,128]{1,0:T(8,128)S(1)}, f32[640,128]{1,0:T(8,128)S(1)}, u32[]{:S(2)}, u32[]{:S(2)}) collective-permute-start(f32[640,128]{1,0:T(8,128)S(1)} %pad_bitcast_fusion), channel_id=1, source_target_pairs={{0,4},{4,8},{8,12},{12,0},{16,20},{20,24},{24,28},{28,16},{32,36},... | collective-permute-start | bytes 983048 | tf_op jit(solution)/shard_map/ppermute | solution.py:38
  57.0 17.6 %collective-permute-start.5 = (f32[640,128]{1,0:T(8,128)S(1)}, f32[640,128]{1,0:T(8,128)S(1)}, u32[]{:S(2)}, u32[]{:S(2)}) collective-permute-start(f32[640,128]{1,0:T(8,128)S(1)} %pad_bitcast_fusion), channel_id=1, source_target_pairs={{0,8},{4,12},{8,0},{12,4},{16,24},{20,28},{24,16},{28,20},{32,40},... | collective-permute-start | bytes 983048 | tf_op jit(solution)/shard_map/ppermute | solution.py:38
  60.4 15.0 %collective-permute-start.6 = (f32[640,128]{1,0:T(8,128)S(1)}, f32[640,128]{1,0:T(8,128)S(1)}, u32[]{:S(2)}, u32[]{:S(2)}) collective-permute-start(f32[640,128]{1,0:T(8,128)S(1)} %pad_bitcast_fusion), channel_id=1, source_target_pairs={{0,12},{4,0},{8,4},{12,8},{16,28},{20,16},{24,20},{28,24},{32,44},... | collective-permute-start | bytes 983048 | tf_op jit(solution)/shard_map/ppermute | solution.py:38
  75.6 13.5 %collective-permute-start.7 = (f32[640,128]{1,0:T(8,128)S(1)}, f32[640,128]{1,0:T(8,128)S(1)}, u32[]{:S(2)}, u32[]{:S(2)}) collective-permute-start(f32[640,128]{1,0:T(8,128)S(1)} %bitcast.278), channel_id=1, source_target_pairs={{0,16},{4,20},{8,24},{12,28},{16,32},{20,36},{24,40},{28,44},{32,4... | collective-permute-start | bytes 983048 | tf_op jit(solution)/shard_map/ppermute | solution.py:38
  77.0 22.4 %collective-permute-start.8 = (f32[640,128]{1,0:T(8,128)S(1)}, f32[640,128]{1,0:T(8,128)S(1)}, u32[]{:S(2)}, u32[]{:S(2)}) collective-permute-start(f32[640,128]{1,0:T(8,128)S(1)} %bitcast.279), channel_id=1, source_target_pairs={{0,32},{4,36},{8,40},{12,44},{16,48},{20,52},{24,56},{28,60},{32,0... | collective-permute-start | bytes 983048 | tf_op jit(solution)/shard_map/ppermute | solution.py:38
  80.7 33.8 %collective-permute-start.2 = (bf16[96,3,128]{2,1,0:T(4,128)(2,1)S(1)}, bf16[96,3,128]{2,1,0:T(4,128)(2,1)S(1)}, u32[]{:S(2)}, u32[]{:S(2)}) collective-permute-start(bf16[96,3,128]{2,1,0:T(4,128)(2,1)S(1)} %get-tuple-element.78), channel_id=1, source_target_pairs={{0,4},{4,8},{8,12},{12,16},{16,20},{20,24},{24,28},{28,32},{32,36}... | collective-permute-start | bytes 221192 | tf_op jit(solution)/shard_map/ppermute | solution.py:25
  82.7 31.8 %collective-permute-start.3 = (bf16[96,3,128]{2,1,0:T(4,128)(2,1)S(1)}, bf16[96,3,128]{2,1,0:T(4,128)(2,1)S(1)}, u32[]{:S(2)}, u32[]{:S(2)}) collective-permute-start(bf16[96,3,128]{2,1,0:T(4,128)(2,1)S(1)} %get-tuple-element.79), channel_id=1, source_target_pairs={{4,0},{8,4},{12,8},{16,12},{20,16},{24,20},{28,24},{32,28},{36,32}... | collective-permute-start | bytes 221192 | tf_op jit(solution)/shard_map/ppermute | solution.py:28
  85.0 25.5 %collective-permute-start.9 = (f32[640,128]{1,0:T(8,128)S(1)}, f32[640,128]{1,0:T(8,128)S(1)}, u32[]{:S(2)}, u32[]{:S(2)}) collective-permute-start(f32[640,128]{1,0:T(8,128)S(1)} %bitcast.280), channel_id=1, source_target_pairs={{0,48},{4,52},{8,56},{12,60},{16,0},{20,4},{24,8},{28,12},{32,16},... | collective-permute-start | bytes 983048 | tf_op jit(solution)/shard_map/ppermute | solution.py:38
  110.6 1.4 copy-start.2
  110.6 1.4 copy-start.5
  110.7 8.0 %collective-permute-start.10 = (f32[640,128]{1,0:T(8,128)S(1)}, f32[640,128]{1,0:T(8,128)S(1)}, u32[]{:S(2)}, u32[]{:S(2)}) collective-permute-start(f32[640,128]{1,0:T(8,128)S(1)} %bitcast.284), channel_id=1, source_target_pairs={{0,64},{4,68},{8,72},{12,76},{16,80},{20,84},{24,88},{28,92},{32,9... | collective-permute-start | bytes 983048 | tf_op jit(solution)/shard_map/ppermute | solution.py:38
  113.0 9.2 %collective-permute-start.11 = (f32[640,128]{1,0:T(8,128)S(1)}, f32[640,128]{1,0:T(8,128)S(1)}, u32[]{:S(2)}, u32[]{:S(2)}) collective-permute-start(f32[640,128]{1,0:T(8,128)S(1)} %bitcast.285), channel_id=1, source_target_pairs={{0,128},{4,132},{8,136},{12,140},{16,144},{20,148},{24,152},{28,15... | collective-permute-start | bytes 983048 | tf_op jit(solution)/shard_map/ppermute | solution.py:38
  115.5 15.6 %collective-permute-start.12 = (f32[640,128]{1,0:T(8,128)S(1)}, f32[640,128]{1,0:T(8,128)S(1)}, u32[]{:S(2)}, u32[]{:S(2)}) collective-permute-start(f32[640,128]{1,0:T(8,128)S(1)} %bitcast.286), channel_id=1, source_target_pairs={{0,192},{4,196},{8,200},{12,204},{16,208},{20,212},{24,216},{28,22... | collective-permute-start | bytes 983048 | tf_op jit(solution)/shard_map/ppermute | solution.py:38
  131.4 16.8 %collective-permute-start.13 = (f32[640,128]{1,0:T(8,128)S(1)}, f32[640,128]{1,0:T(8,128)S(1)}, u32[]{:S(2)}, u32[]{:S(2)}) collective-permute-start(f32[640,128]{1,0:T(8,128)S(1)} %bitcast.281), channel_id=1, source_target_pairs={{0,1},{1,2},{2,3},{3,0},{4,5},{5,6},{6,7},{7,4},{8,9},{9,10},{10,1... | collective-permute-start | bytes 983048 | tf_op jit(solution)/shard_map/ppermute | solution.py:38
  132.7 17.0 %collective-permute-start.14 = (f32[640,128]{1,0:T(8,128)S(1)}, f32[640,128]{1,0:T(8,128)S(1)}, u32[]{:S(2)}, u32[]{:S(2)}) collective-permute-start(f32[640,128]{1,0:T(8,128)S(1)} %bitcast.282), channel_id=1, source_target_pairs={{0,2},{1,3},{2,0},{3,1},{4,6},{5,7},{6,4},{7,5},{8,10},{9,11},{10,... | collective-permute-start | bytes 983048 | tf_op jit(solution)/shard_map/ppermute | solution.py:38
  147.1 8.2 %collective-permute-start.15 = (f32[640,128]{1,0:T(8,128)S(1)}, f32[640,128]{1,0:T(8,128)S(1)}, u32[]{:S(2)}, u32[]{:S(2)}) collective-permute-start(f32[640,128]{1,0:T(8,128)S(1)} %bitcast.283), channel_id=1, source_target_pairs={{0,3},{1,0},{2,1},{3,2},{4,7},{5,4},{6,5},{7,6},{8,11},{9,8},{10,9... | collective-permute-start | bytes 983048 | tf_op jit(solution)/shard_map/ppermute | solution.py:38

commit v3 on v1

--- a/solution.py
+++ b/solution.py
@@ -55,7 +55,9 @@
     rows += (-rows) % 128
     block = jnp.pad(flat, (0, rows * lanes - flat.shape[0])).reshape(rows, lanes)
     steps = []
-    for number, (axis, stride, radix) in enumerate(digit_groups(axes)):
+    groups = digit_groups(axes)
+    groups = [groups[1], groups[0]] + groups[2:]
+    for number, (axis, stride, radix) in enumerate(groups):
         digit = (lax.axis_index(axis) // stride) % radix
         height, rest = divmod(block.shape[0], radix)
         if rest or number >= halvings:

time: 126 us -> 132 us (1.048)
  waiting for transfers between devices: 20.4 us -> 24.6 us
  starting transfers between devices: 37.8 us -> 39.3 us
    ppermute x15, waiting for transfers between devices: 20.4 us -> 24.6 us  [shifted(): return lax.ppermute(values, axis, pairs)]
    ppermute x15, starting transfers between devices: 27.2 us -> 28.8 us  [shifted(): return lax.ppermute(values, axis, pairs)]
where the time goes in v3:
time: 132 us; the launch traced here: 131 us
  other arithmetic  52.3 us (40%)
  starting transfers between devices  39.3 us (30%)
  waiting for transfers between devices  24.6 us (19%)
  local copies, waits for them, and re-layouts  8.73 us (7%)
  matrix products  4.65 us (4%)
    ppermute x15, starting transfers between devices, shifted(): return lax.ppermute(values, axis, pairs)  28.8 us
    ppermute x15, waiting for transfers between devices, shifted(): return lax.ppermute(values, axis, pairs)  24.6 us
    reduce_sum x4, other arithmetic, kernel_sums(): entries.append(jnp.sum(grad_f * piece, axis=(1, 2)))  19.6 us
    broadcast_in_dim x1, other arithmetic, on_device(): grad_image[None]  11.8 us
    reduce_sum x1, other arithmetic, on_device(): centered = pre - jnp.mean(pre, axis=0, keepdims=True)  11.6 us
    ppermute x2, starting transfers between devices, extended(): lax.ppermute(lax.slice_in_dim(block, block.shape[dim] - width, None, axis...  6.03 us
    ppermute x2, starting transfers between devices, extended(): lax.ppermute(lax.slice_in_dim(block, 0, width, axis=dim), axis, backward)  4.41 us
    mul x3, local copies, waits for them, and re-layouts, depthwise(): weight * padded[:, k_row:k_row + strip_w, k_col:k_col + strip_h].astype(j...  2.93 us
  transfers between devices with their start and end apart: 19, of which 10 were waited for; matrix products, arithmetic and copies ran while one was open for 15% of the time, Pallas kernels for 0%

profile of v3, /device:TPU:3, one launch (start us, length us, event | category | flops | bytes accessed | tf_op | source)
XLA Modules:
  0.0 130.8 jit_solution(5610890093270690639)
XLA Ops:
  0.7 0.7 convert_bitcast_fusion
  1.5 1.0 bitcast_multiply_fusion.5
  2.6 4.1 %collective-permute-start = (bf16[96,3,128]{2,1,0:T(4,128)(2,1)S(1)}, bf16[96,3,128]{2,1,0:T(4,128)(2,1)S(1)}, u32[]{:S(2)}, u32[]{:S(2)}) collective-permute-start(bf16[96,3,128]{2,1,0:T(4,128)(2,1)S(1)} %get-tuple-element.82), channel_id=1, source_target_pairs={{0,4},{4,8},{8,12},{12,16},{16,20},{20,24},{24,28},{28,32},{32,36}... | collective-permute-start | bytes 221192 | tf_op jit(solution)/shard_map/ppermute | solution.py:25
  6.8 1.9 %collective-permute-start.1 = (bf16[96,3,128]{2,1,0:T(4,128)(2,1)S(1)}, bf16[96,3,128]{2,1,0:T(4,128)(2,1)S(1)}, u32[]{:S(2)}, u32[]{:S(2)}) collective-permute-start(bf16[96,3,128]{2,1,0:T(4,128)(2,1)S(1)} %get-tuple-element.83), channel_id=1, source_target_pairs={{4,0},{8,4},{12,8},{16,12},{20,16},{24,20},{28,24},{32,28},{36,32}... | collective-permute-start | bytes 221192 | tf_op jit(solution)/shard_map/ppermute | solution.py:28
  8.8 1.0 slice_bitcast_fusion.48
  9.8 1.0 slice_bitcast_fusion.47
  10.8 0.9 slice_bitcast_fusion.46
  11.7 1.2 fusion.19
  12.9 0.8 convert_reduce_fusion.3
  13.7 1.0 select_maximum_fusion.2
  14.8 11.6 %fusion.171 = (f32[16,128]{1,0:T(8,128)S(1)}, f32[96,16,128]{2,1,0:T(8,128)S(1)}) fusion(f32[96]{0:T(128)S(1)} %copy-done.7, bf16[96,22,134]{2,1,0:T(8,128)(2,1)S(1)} %select_maximum_fusion.2, f32[96]{0:T(128)S(1)} %get-tuple-element.134, f32[96]{0:T(128)S(1)} %get-tuple-element.135, f32[96]{0:T(128)S(1)} %get-tuple-element.88, ...), kind=kLoop, calls=%fused_computation.409 | loop fusion | flops 32634880 | bytes 17869568 | tf_op jit(solution)/shard_map/reduce_sum | solution.py:187
  26.9 1.0 fusion.7
  27.8 1.6 %fusion.5 = bf16[384,2048]{0,1:T(8,128)(2,1)S(1)} fusion(f32[2048,384]{1,0:T(8,128)S(1)} %get-tuple-element.137, bf16[96,384]{1,0:T(8,128)(2,1)S(1)} %copy-done.3, bf16[12,8,16,128]{3,2,1,0:T(8,128)(2,1)S(1)} %bitcast.266), kind=kOutput, calls=%fused_computation.59 | convolution fusion | flops 158859264 | bytes 5185536 | tf_op jit(solution)/shard_map/cf,cp->fp/dot_general | solution.py:150
  30.9 1.2 fusion.73
  32.6 7.6 %fusion.149 = (f32[96]{0:T(128)S(1)}, f32[96]{0:T(128)S(1)}, f32[96]{0:T(128)S(1)}, f32[96]{0:T(128)S(1)}, f32[96]{0:T(128)S(1)}, /*index=5*/f32[96]{0:T(128)S(1...) fusion(bf16[96,16,128]{2,1,0:T(8,128)(2,1)S(1)} %fusion.23, ...), kind=kLoop, calls=%fused_computation.270 | loop fusion | flops 10811712 | bytes 7478016 | tf_op jit(solution)/shard_map/reduce_sum | solution.py:127
  40.2 7.6 %fusion.150 = (f32[96]{0:T(128)S(1)}, f32[96]{0:T(128)S(1)}, f32[96]{0:T(128)S(1)}, f32[96]{0:T(128)S(1)}, f32[96]{0:T(128)S(1)}, /*index=5*/f32[96]{0:T(128)S(1...) fusion(bf16[96,16,128]{2,1,0:T(8,128)(2,1)S(1)} %fusion.23, ...), kind=kLoop, calls=%fused_computation.271 | loop fusion | flops 10811712 | bytes 7478016 | tf_op jit(solution)/shard_map/reduce_sum | solution.py:127
  47.8 2.1 %fusion.148 = (f32[96]{0:T(128)S(1)}, f32[96]{0:T(128)S(1)}, f32[96]{0:T(128)S(1)}, f32[96]{0:T(128)S(1)}, f32[96]{0:T(128)S(1)}, /*index=5*/f32[96]{0:T(128)S(1)}) fusion(bf16[96,16,128]{2,1,0:T(8,128)(2,1)S(1)} %fusion.23, bf16[96,22,134]{2,1,0:T(8,128)(2,1)S(1)} %select_maximum_fusion.2), kind=kLoop, calls=%fused_computation.269 | loop fusion | flops 3734976 | bytes 2754816 | tf_op jit(solution)/shard_map/reduce_sum | solution.py:127
  51.1 2.3 %fusion.147 = (f32[96]{0:T(128)S(1)}, f32[96]{0:T(128)S(1)}, f32[96]{0:T(128)S(1)}, f32[96]{0:T(128)S(1)}, f32[96]{0:T(128)S(1)}, /*index=5*/f32[96]{0:T(128)S(1)}, f32[96]{0:T(128)S(1)}, f32[96]{0:T(128)S(1)}) fusion(bf16[96,16,128]{2,1,0:T(8,128)(2,1)S(1)} %fusion.23, bf16[96,3,128]{2,1,0:T(4,128)(2,1)S(1)} %collective-permute-done.1, ...), kind=kLoop, calls=%fused_computation.268 | loop fusion | flops 8060160 | bytes 936960 | tf_op jit(solution)/shard_map/reduce_sum | solution.py:127
  54.0 1.4 %concatenate.35 = f32[79296]{0:T(1024)S(1)} concatenate(f32[73728]{0:T(1024)S(1)} %mul.1410, f32[4704]{0:T(1024)S(1)} %mul.1462, f32[480]{0:T(512)S(1)} %mul.1468, f32[384]{0:T(512)S(1)} %broadcast_multiply_fusion.4), dimensions={0} | concatenate | bytes 634368 | tf_op jit(solution)/shard_map/concatenate | solution.py:53
  55.5 3.1 %collective-permute-start.4 = (f32[160,128]{1,0:T(8,128)S(1)}, f32[160,128]{1,0:T(8,128)S(1)}, u32[]{:S(2)}, u32[]{:S(2)}) collective-permute-start(f32[160,128]{1,0:T(8,128)S(1)} %get-tuple-element.84), channel_id=1, source_target_pairs={{0,16},{4,20},{8,24},{12,28},{16,32},{20,36},{24,40},{28,44},{32,4... | collective-permute-start | bytes 245768 | tf_op jit(solution)/shard_map/ppermute | solution.py:38
  58.6 4.2 %collective-permute-start.5 = (f32[160,128]{1,0:T(8,128)S(1)}, f32[160,128]{1,0:T(8,128)S(1)}, u32[]{:S(2)}, u32[]{:S(2)}) collective-permute-start(f32[160,128]{1,0:T(8,128)S(1)} %get-tuple-element.86), channel_id=1, source_target_pairs={{0,32},{4,36},{8,40},{12,44},{16,48},{20,52},{24,56},{28,60},{32,0... | collective-permute-start | bytes 245768 | tf_op jit(solution)/shard_map/ppermute | solution.py:38
  62.8 2.4 %collective-permute-start.6 = (f32[160,128]{1,0:T(8,128)S(1)}, f32[160,128]{1,0:T(8,128)S(1)}, u32[]{:S(2)}, u32[]{:S(2)}) collective-permute-start(f32[160,128]{1,0:T(8,128)S(1)} %get-tuple-element.85), channel_id=1, source_target_pairs={{0,48},{4,52},{8,56},{12,60},{16,0},{20,4},{24,8},{28,12},{32,16},... | collective-permute-start | bytes 245768 | tf_op jit(solution)/shard_map/ppermute | solution.py:38
  65.2 1.9 %collective-permute-done.5 = f32[160,128]{1,0:T(8,128)S(1)} collective-permute-done((f32[160,128]{1,0:T(8,128)S(1)}, f32[160,128]{1,0:T(8,128)S(1)}, u32[]{:S(2)}, u32[]{:S(2)}) %collective-permute-start.5) | collective-permute-done | bytes 81952 | tf_op jit(solution)/shard_map/ppermute | solution.py:38
  67.1 5.0 %collective-permute-done.6 = f32[160,128]{1,0:T(8,128)S(1)} collective-permute-done((f32[160,128]{1,0:T(8,128)S(1)}, f32[160,128]{1,0:T(8,128)S(1)}, u32[]{:S(2)}, u32[]{:S(2)}) %collective-permute-start.6) | collective-permute-done | bytes 81952 | tf_op jit(solution)/shard_map/ppermute | solution.py:38
  72.4 1.9 %collective-permute-start.2 = (bf16[96,3,128]{2,1,0:T(4,128)(2,1)S(1)}, bf16[96,3,128]{2,1,0:T(4,128)(2,1)S(1)}, u32[]{:S(2)}, u32[]{:S(2)}) collective-permute-start(bf16[96,3,128]{2,1,0:T(4,128)(2,1)S(1)} %get-tuple-element.80), channel_id=1, source_target_pairs={{0,4},{4,8},{8,12},{12,16},{16,20},{20,24},{24,28},{28,32},{32,36}... | collective-permute-start | bytes 221192 | tf_op jit(solution)/shard_map/ppermute | solution.py:25
  74.3 2.5 %collective-permute-start.3 = (bf16[96,3,128]{2,1,0:T(4,128)(2,1)S(1)}, bf16[96,3,128]{2,1,0:T(4,128)(2,1)S(1)}, u32[]{:S(2)}, u32[]{:S(2)}) collective-permute-start(bf16[96,3,128]{2,1,0:T(4,128)(2,1)S(1)} %get-tuple-element.81), channel_id=1, source_target_pairs={{4,0},{8,4},{12,8},{16,12},{20,16},{24,20},{28,24},{32,28},{36,32}... | collective-permute-start | bytes 221192 | tf_op jit(solution)/shard_map/ppermute | solution.py:28
  76.8 2.7 %collective-permute-start.8 = (f32[160,128]{1,0:T(8,128)S(1)}, f32[160,128]{1,0:T(8,128)S(1)}, u32[]{:S(2)}, u32[]{:S(2)}) collective-permute-start(f32[160,128]{1,0:T(8,128)S(1)} %get-tuple-element.77), channel_id=1, source_target_pairs={{0,8},{4,12},{8,0},{12,4},{16,24},{20,28},{24,16},{28,20},{32,40},... | collective-permute-start | bytes 245768 | tf_op jit(solution)/shard_map/ppermute | solution.py:38
  79.5 1.3 %collective-permute-start.9 = (f32[160,128]{1,0:T(8,128)S(1)}, f32[160,128]{1,0:T(8,128)S(1)}, u32[]{:S(2)}, u32[]{:S(2)}) collective-permute-start(f32[160,128]{1,0:T(8,128)S(1)} %get-tuple-element.77), channel_id=1, source_target_pairs={{0,12},{4,0},{8,4},{12,8},{16,28},{20,16},{24,20},{28,24},{32,44},... | collective-permute-start | bytes 245768 | tf_op jit(solution)/shard_map/ppermute | solution.py:38
  80.8 0.8 collective-permute-done.8
  81.7 3.7 %collective-permute-done.9 = f32[160,128]{1,0:T(8,128)S(1)} collective-permute-done((f32[160,128]{1,0:T(8,128)S(1)}, f32[160,128]{1,0:T(8,128)S(1)}, u32[]{:S(2)}, u32[]{:S(2)}) %collective-permute-start.9) | collective-permute-done | bytes 81952 | tf_op jit(solution)/shard_map/ppermute | solution.py:38
  85.4 1.3 collective-permute-start.10
  86.7 1.0 multiply_convert_fusion
  88.4 2.0 %collective-permute-start.12 = (f32[160,128]{1,0:T(8,128)S(1)}, f32[160,128]{1,0:T(8,128)S(1)}, u32[]{:S(2)}, u32[]{:S(2)}) collective-permute-start(f32[160,128]{1,0:T(8,128)S(1)} %bitcast.281), channel_id=1, source_target_pairs={{0,192},{4,196},{8,200},{12,204},{16,208},{20,212},{24,216},{28,22... | collective-permute-start | bytes 245768 | tf_op jit(solution)/shard_map/ppermute | solution.py:38
  90.4 2.7 %collective-permute-done.11 = f32[160,128]{1,0:T(8,128)S(1)} collective-permute-done((f32[160,128]{1,0:T(8,128)S(1)}, f32[160,128]{1,0:T(8,128)S(1)}, u32[]{:S(2)}, u32[]{:S(2)}) %collective-permute-start.11) | collective-permute-done | bytes 81952 | tf_op jit(solution)/shard_map/ppermute | solution.py:38
  93.8 1.4 %collective-permute-start.13 = (f32[160,128]{1,0:T(8,128)S(1)}, f32[160,128]{1,0:T(8,128)S(1)}, u32[]{:S(2)}, u32[]{:S(2)}) collective-permute-start(f32[160,128]{1,0:T(8,128)S(1)} %bitcast.276), channel_id=1, source_target_pairs={{0,1},{1,2},{2,3},{3,0},{4,5},{5,6},{6,7},{7,4},{8,9},{9,10},{10,1... | collective-permute-start | bytes 245768 | tf_op jit(solution)/shard_map/ppermute | solution.py:38
  95.2 1.0 select_maximum_fusion
  96.2 2.7 %collective-permute-start.14 = (f32[160,128]{1,0:T(8,128)S(1)}, f32[160,128]{1,0:T(8,128)S(1)}, u32[]{:S(2)}, u32[]{:S(2)}) collective-permute-start(f32[160,128]{1,0:T(8,128)S(1)} %bitcast.277), channel_id=1, source_target_pairs={{0,2},{1,3},{2,0},{3,1},{4,6},{5,7},{6,4},{7,5},{8,10},{9,11},{10,... | collective-permute-start | bytes 245768 | tf_op jit(solution)/shard_map/ppermute | solution.py:38
  98.9 1.1 collective-permute-start.15
  100.0 1.7 %collective-permute-done.14 = f32[160,128]{1,0:T(8,128)S(1)} collective-permute-done((f32[160,128]{1,0:T(8,128)S(1)}, f32[160,128]{1,0:T(8,128)S(1)}, u32[]{:S(2)}, u32[]{:S(2)}) %collective-permute-start.14) | collective-permute-done | bytes 81952 | tf_op jit(solution)/shard_map/ppermute | solution.py:38
  101.7 1.6 %collective-permute-done.15 = f32[160,128]{1,0:T(8,128)S(1)} collective-permute-done((f32[160,128]{1,0:T(8,128)S(1)}, f32[160,128]{1,0:T(8,128)S(1)}, u32[]{:S(2)}, u32[]{:S(2)}) %collective-permute-start.15) | collective-permute-done | bytes 81952 | tf_op jit(solution)/shard_map/ppermute | solution.py:38
  103.8 11.8 %fusion.164 = bf16[1,96,16,128]{3,2,1,0:T(8,128)(2,1)} fusion(bf16[96,22,134]{2,1,0:T(8,128)(2,1)S(1)} %select_maximum_fusion, f32[96]{0:T(128)S(1)} %get-tuple-element.87, f32[96]{0:T(128)S(1)} %get-tuple-element.106, f32[96]{0:T(128)S(1)} %get-tuple-element.125, bf16[96,3,128]{2,1,0:T(4,128)(2,1)S(1)} %collective-permute-done.3, ...), kind=kLoop, calls=%fused_computation.314 | loop fusion | flops 33030144 | bytes 17861504 | tf_op jit(solution)/shard_map/broadcast_in_dim | solution.py:233
  115.6 2.2 %collective-permute-start.17 = (f32[160,128]{1,0:T(8,128)S(1)}, f32[160,128]{1,0:T(8,128)S(1)}, u32[]{:S(2)}, u32[]{:S(2)}) collective-permute-start(f32[160,128]{1,0:T(8,128)S(1)} %get-tuple-element.71), channel_id=1, source_target_pairs={{0,32},{4,36},{8,40},{12,44},{16,48},{20,52},{24,56},{28,60},{32,0... | collective-permute-start | bytes 245768 | tf_op jit(solution)/shard_map/ppermute | solution.py:38
  117.7 3.3 %collective-permute-start.18 = (f32[160,128]{1,0:T(8,128)S(1)}, f32[160,128]{1,0:T(8,128)S(1)}, u32[]{:S(2)}, u32[]{:S(2)}) collective-permute-start(f32[160,128]{1,0:T(8,128)S(1)} %get-tuple-element.71), channel_id=1, source_target_pairs={{0,48},{4,52},{8,56},{12,60},{16,0},{20,4},{24,8},{28,12},{32,16},... | collective-permute-start | bytes 245768 | tf_op jit(solution)/shard_map/ppermute | solution.py:38
  121.1 1.8 %collective-permute-done.17 = f32[160,128]{1,0:T(8,128)S(1)} collective-permute-done((f32[160,128]{1,0:T(8,128)S(1)}, f32[160,128]{1,0:T(8,128)S(1)}, u32[]{:S(2)}, u32[]{:S(2)}) %collective-permute-start.17) | collective-permute-done | bytes 81952 | tf_op jit(solution)/shard_map/ppermute | solution.py:38
  122.9 4.9 %collective-permute-done.18 = f32[160,128]{1,0:T(8,128)S(1)} collective-permute-done((f32[160,128]{1,0:T(8,128)S(1)}, f32[160,128]{1,0:T(8,128)S(1)}, u32[]{:S(2)}, u32[]{:S(2)}) %collective-permute-start.18) | collective-permute-done | bytes 81952 | tf_op jit(solution)/shard_map/ppermute | solution.py:38
  128.5 0.8 reshape.231
  129.5 0.7 copy.19
  130.2 0.7 reshape.234
  (91 shorter events, 7.4 us)
Async XLA Ops:
  0.6 26.2 %copy-start = (bf16[96,384]{1,0:T(8,128)(2,1)S(1)}, bf16[96,384]{1,0:T(8,128)(2,1)}, u32[]{:S(2)}) copy-start(bf16[96,384]{1,0:T(8,128)(2,1)} %param.19) | copy-start | bytes 221188
  0.6 14.1 %copy-start.7 = (f32[96]{0:T(128)S(1)}, f32[96]{0:T(128)}, u32[]{:S(2)}) copy-start(f32[96]{0:T(128)} %param.16) | copy-start | bytes 1156
  2.6 11.1 %collective-permute-start = (bf16[96,3,128]{2,1,0:T(4,128)(2,1)S(1)}, bf16[96,3,128]{2,1,0:T(4,128)(2,1)S(1)}, u32[]{:S(2)}, u32[]{:S(2)}) collective-permute-start(bf16[96,3,128]{2,1,0:T(4,128)(2,1)S(1)} %get-tuple-element.82), channel_id=1, source_target_pairs={{0,4},{4,8},{8,12},{12,16},{16,20},{20,24},{24,28},{28,32},{32,36}... | collective-permute-start | bytes 221192 | tf_op jit(solution)/shard_map/ppermute | solution.py:25
  6.8 7.0 %collective-permute-start.1 = (bf16[96,3,128]{2,1,0:T(4,128)(2,1)S(1)}, bf16[96,3,128]{2,1,0:T(4,128)(2,1)S(1)}, u32[]{:S(2)}, u32[]{:S(2)}) collective-permute-start(bf16[96,3,128]{2,1,0:T(4,128)(2,1)S(1)} %get-tuple-element.83), channel_id=1, source_target_pairs={{4,0},{8,4},{12,8},{16,12},{20,16},{24,20},{28,24},{32,28},{36,32}... | collective-permute-start | bytes 221192 | tf_op jit(solution)/shard_map/ppermute | solution.py:28
  14.8 11.8 %copy-start.4 = (f32[96]{0:T(128)S(1)}, f32[96]{0:T(128)}, u32[]{:S(2)}) copy-start(f32[96]{0:T(128)} %param.17) | copy-start | bytes 1156
  14.8 11.7 %copy-start.8 = (f32[96]{0:T(128)S(1)}, f32[96]{0:T(128)}, u32[]{:S(2)}) copy-start(f32[96]{0:T(128)} %param.18) | copy-start | bytes 1156
  14.8 12.0 %copy-start.6 = (f32[384]{0:T(512)S(1)}, f32[384]{0:T(512)}, u32[]{:S(2)}) copy-start(f32[384]{0:T(512)} %param.20) | copy-start | bytes 4612
  26.9 1.0 copy-start.3
  29.5 0.7 copy-start.9
  29.5 1.4 %copy-start.1 = (bf16[1,96,16,128]{3,2,1,0:T(8,128)(2,1)S(1)}, bf16[1,96,16,128]{3,2,1,0:T(8,128)(2,1)}, u32[]{:S(2)}) copy-start(bf16[1,96,16,128]{3,2,1,0:T(8,128)(2,1)} %param.13) | copy-start | bytes 1179652
  54.0 32.7 %copy-start.2 = (bf16[1,96,16,128]{3,2,1,0:T(8,128)(2,1)S(1)}, bf16[1,96,16,128]{3,2,1,0:T(8,128)(2,1)}, u32[]{:S(2)}) copy-start(bf16[1,96,16,128]{3,2,1,0:T(8,128)(2,1)} %param.12) | copy-start | bytes 1179652
  54.0 32.7 %copy-start.5 = (f32[96]{0:T(128)S(1)}, f32[96]{0:T(128)}, u32[]{:S(2)}) copy-start(f32[96]{0:T(128)} %param.23) | copy-start | bytes 1156
  55.5 9.7 %collective-permute-start.4 = (f32[160,128]{1,0:T(8,128)S(1)}, f32[160,128]{1,0:T(8,128)S(1)}, u32[]{:S(2)}, u32[]{:S(2)}) collective-permute-start(f32[160,128]{1,0:T(8,128)S(1)} %get-tuple-element.84), channel_id=1, source_target_pairs={{0,16},{4,20},{8,24},{12,28},{16,32},{20,36},{24,40},{28,44},{32,4... | collective-permute-start | bytes 245768 | tf_op jit(solution)/shard_map/ppermute | solution.py:38
  58.6 8.5 %collective-permute-start.5 = (f32[160,128]{1,0:T(8,128)S(1)}, f32[160,128]{1,0:T(8,128)S(1)}, u32[]{:S(2)}, u32[]{:S(2)}) collective-permute-start(f32[160,128]{1,0:T(8,128)S(1)} %get-tuple-element.86), channel_id=1, source_target_pairs={{0,32},{4,36},{8,40},{12,44},{16,48},{20,52},{24,56},{28,60},{32,0... | collective-permute-start | bytes 245768 | tf_op jit(solution)/shard_map/ppermute | solution.py:38
  62.8 9.3 %collective-permute-start.6 = (f32[160,128]{1,0:T(8,128)S(1)}, f32[160,128]{1,0:T(8,128)S(1)}, u32[]{:S(2)}, u32[]{:S(2)}) collective-permute-start(f32[160,128]{1,0:T(8,128)S(1)} %get-tuple-element.85), channel_id=1, source_target_pairs={{0,48},{4,52},{8,56},{12,60},{16,0},{20,4},{24,8},{28,12},{32,16},... | collective-permute-start | bytes 245768 | tf_op jit(solution)/shard_map/ppermute | solution.py:38
  72.2 8.6 %collective-permute-start.7 = (f32[160,128]{1,0:T(8,128)S(1)}, f32[160,128]{1,0:T(8,128)S(1)}, u32[]{:S(2)}, u32[]{:S(2)}) collective-permute-start(f32[160,128]{1,0:T(8,128)S(1)} %get-tuple-element.77), channel_id=1, source_target_pairs={{0,4},{4,8},{8,12},{12,0},{16,20},{20,24},{24,28},{28,16},{32,36},... | collective-permute-start | bytes 245768 | tf_op jit(solution)/shard_map/ppermute | solution.py:38
  72.4 22.8 %collective-permute-start.2 = (bf16[96,3,128]{2,1,0:T(4,128)(2,1)S(1)}, bf16[96,3,128]{2,1,0:T(4,128)(2,1)S(1)}, u32[]{:S(2)}, u32[]{:S(2)}) collective-permute-start(bf16[96,3,128]{2,1,0:T(4,128)(2,1)S(1)} %get-tuple-element.80), channel_id=1, source_target_pairs={{0,4},{4,8},{8,12},{12,16},{16,20},{20,24},{24,28},{28,32},{32,36}... | collective-permute-start | bytes 221192 | tf_op jit(solution)/shard_map/ppermute | solution.py:25
  74.3 20.9 %collective-permute-start.3 = (bf16[96,3,128]{2,1,0:T(4,128)(2,1)S(1)}, bf16[96,3,128]{2,1,0:T(4,128)(2,1)S(1)}, u32[]{:S(2)}, u32[]{:S(2)}) collective-permute-start(bf16[96,3,128]{2,1,0:T(4,128)(2,1)S(1)} %get-tuple-element.81), channel_id=1, source_target_pairs={{4,0},{8,4},{12,8},{16,12},{20,16},{24,20},{28,24},{32,28},{36,32}... | collective-permute-start | bytes 221192 | tf_op jit(solution)/shard_map/ppermute | solution.py:28
  76.8 4.9 %collective-permute-start.8 = (f32[160,128]{1,0:T(8,128)S(1)}, f32[160,128]{1,0:T(8,128)S(1)}, u32[]{:S(2)}, u32[]{:S(2)}) collective-permute-start(f32[160,128]{1,0:T(8,128)S(1)} %get-tuple-element.77), channel_id=1, source_target_pairs={{0,8},{4,12},{8,0},{12,4},{16,24},{20,28},{24,16},{28,20},{32,40},... | collective-permute-start | bytes 245768 | tf_op jit(solution)/shard_map/ppermute | solution.py:38
  79.5 5.9 %collective-permute-start.9 = (f32[160,128]{1,0:T(8,128)S(1)}, f32[160,128]{1,0:T(8,128)S(1)}, u32[]{:S(2)}, u32[]{:S(2)}) collective-permute-start(f32[160,128]{1,0:T(8,128)S(1)} %get-tuple-element.77), channel_id=1, source_target_pairs={{0,12},{4,0},{8,4},{12,8},{16,28},{20,16},{24,20},{28,24},{32,44},... | collective-permute-start | bytes 245768 | tf_op jit(solution)/shard_map/ppermute | solution.py:38
  85.4 5.0 %collective-permute-start.10 = (f32[160,128]{1,0:T(8,128)S(1)}, f32[160,128]{1,0:T(8,128)S(1)}, u32[]{:S(2)}, u32[]{:S(2)}) collective-permute-start(f32[160,128]{1,0:T(8,128)S(1)} %bitcast.279), channel_id=1, source_target_pairs={{0,64},{4,68},{8,72},{12,76},{16,80},{20,84},{24,88},{28,92},{32,9... | collective-permute-start | bytes 245768 | tf_op jit(solution)/shard_map/ppermute | solution.py:38
  87.7 5.4 %collective-permute-start.11 = (f32[160,128]{1,0:T(8,128)S(1)}, f32[160,128]{1,0:T(8,128)S(1)}, u32[]{:S(2)}, u32[]{:S(2)}) collective-permute-start(f32[160,128]{1,0:T(8,128)S(1)} %bitcast.280), channel_id=1, source_target_pairs={{0,128},{4,132},{8,136},{12,140},{16,144},{20,148},{24,152},{28,15... | collective-permute-start | bytes 245768 | tf_op jit(solution)/shard_map/ppermute | solution.py:38
  88.4 5.3 %collective-permute-start.12 = (f32[160,128]{1,0:T(8,128)S(1)}, f32[160,128]{1,0:T(8,128)S(1)}, u32[]{:S(2)}, u32[]{:S(2)}) collective-permute-start(f32[160,128]{1,0:T(8,128)S(1)} %bitcast.281), channel_id=1, source_target_pairs={{0,192},{4,196},{8,200},{12,204},{16,208},{20,212},{24,216},{28,22... | collective-permute-start | bytes 245768 | tf_op jit(solution)/shard_map/ppermute | solution.py:38
  93.8 6.2 %collective-permute-start.13 = (f32[160,128]{1,0:T(8,128)S(1)}, f32[160,128]{1,0:T(8,128)S(1)}, u32[]{:S(2)}, u32[]{:S(2)}) collective-permute-start(f32[160,128]{1,0:T(8,128)S(1)} %bitcast.276), channel_id=1, source_target_pairs={{0,1},{1,2},{2,3},{3,0},{4,5},{5,6},{6,7},{7,4},{8,9},{9,10},{10,1... | collective-permute-start | bytes 245768 | tf_op jit(solution)/shard_map/ppermute | solution.py:38
  96.2 5.5 %collective-permute-start.14 = (f32[160,128]{1,0:T(8,128)S(1)}, f32[160,128]{1,0:T(8,128)S(1)}, u32[]{:S(2)}, u32[]{:S(2)}) collective-permute-start(f32[160,128]{1,0:T(8,128)S(1)} %bitcast.277), channel_id=1, source_target_pairs={{0,2},{1,3},{2,0},{3,1},{4,6},{5,7},{6,4},{7,5},{8,10},{9,11},{10,... | collective-permute-start | bytes 245768 | tf_op jit(solution)/shard_map/ppermute | solution.py:38
  98.9 4.4 %collective-permute-start.15 = (f32[160,128]{1,0:T(8,128)S(1)}, f32[160,128]{1,0:T(8,128)S(1)}, u32[]{:S(2)}, u32[]{:S(2)}) collective-permute-start(f32[160,128]{1,0:T(8,128)S(1)} %bitcast.278), channel_id=1, source_target_pairs={{0,3},{1,0},{2,1},{3,2},{4,7},{5,4},{6,5},{7,6},{8,11},{9,8},{10,9... | collective-permute-start | bytes 245768 | tf_op jit(solution)/shard_map/ppermute | solution.py:38
  103.4 17.7 %collective-permute-start.16 = (f32[160,128]{1,0:T(8,128)S(1)}, f32[160,128]{1,0:T(8,128)S(1)}, u32[]{:S(2)}, u32[]{:S(2)}) collective-permute-start(f32[160,128]{1,0:T(8,128)S(1)} %get-tuple-element.71), channel_id=1, source_target_pairs={{0,16},{4,20},{8,24},{12,28},{16,32},{20,36},{24,40},{28,44},{32,4... | collective-permute-start | bytes 245768 | tf_op jit(solution)/shard_map/ppermute | solution.py:38
  115.6 7.3 %collective-permute-start.17 = (f32[160,128]{1,0:T(8,128)S(1)}, f32[160,128]{1,0:T(8,128)S(1)}, u32[]{:S(2)}, u32[]{:S(2)}) collective-permute-start(f32[160,128]{1,0:T(8,128)S(1)} %get-tuple-element.71), channel_id=1, source_target_pairs={{0,32},{4,36},{8,40},{12,44},{16,48},{20,52},{24,56},{28,60},{32,0... | collective-permute-start | bytes 245768 | tf_op jit(solution)/shard_map/ppermute | solution.py:38
  117.7 10.0 %collective-permute-start.18 = (f32[160,128]{1,0:T(8,128)S(1)}, f32[160,128]{1,0:T(8,128)S(1)}, u32[]{:S(2)}, u32[]{:S(2)}) collective-permute-start(f32[160,128]{1,0:T(8,128)S(1)} %get-tuple-element.71), channel_id=1, source_target_pairs={{0,48},{4,52},{8,56},{12,60},{16,0},{20,4},{24,8},{28,12},{32,16},... | collective-permute-start | bytes 245768 | tf_op jit(solution)/shard_map/ppermute | solution.py:38

commit v4 on v1

--- a/solution.py
+++ b/solution.py
@@ -52,7 +52,7 @@
 def summed_everywhere(parts, axes, lanes=128, halvings=1):
     flat = jnp.concatenate([p.reshape(-1) for p in parts])
     rows = -(-flat.shape[0] // lanes)
-    rows += (-rows) % 128
+    rows += (-rows) % 4
     block = jnp.pad(flat, (0, rows * lanes - flat.shape[0])).reshape(rows, lanes)
     steps = []
     for number, (axis, stride, radix) in enumerate(digit_groups(axes)):

time: 126 us -> 125 us (level)
  waiting for transfers between devices: 20.4 us -> 16.6 us
  local copies, waits for them, and re-layouts: 8.73 us -> 11.2 us
    ppermute x15, waiting for transfers between devices: 20.4 us -> 16.6 us  [shifted(): return lax.ppermute(values, axis, pairs)]
    dynamic_update_slice x3, local copies, waits for them, and re-layouts: 0.03 us -> 1.82 us  [summed_everywhere(): lax.dynamic_update_slice_in_dim(whole, got, (digit - shift) % radix * hei...]
  transfers between devices with their start and end apart: 19 -> 19, of which waited for: 10 -> 8; matrix products, arithmetic and copies ran while one was open for 15% -> 17% of each run, Pallas kernels for 0% -> 0%
where the time goes in v4:
time: 125 us; the launch traced here: 124 us
  other arithmetic  52.3 us (42%)
  starting transfers between devices  37.8 us (30%)
  waiting for transfers between devices  16.6 us (13%)
  local copies, waits for them, and re-layouts  11.2 us (9%)
  matrix products  4.65 us (4%)
  between operations  1.28 us (1%)
    ppermute x15, starting transfers between devices, shifted(): return lax.ppermute(values, axis, pairs)  27.2 us
    reduce_sum x4, other arithmetic, kernel_sums(): entries.append(jnp.sum(grad_f * piece, axis=(1, 2)))  19.6 us
    ppermute x15, waiting for transfers between devices, shifted(): return lax.ppermute(values, axis, pairs)  16.6 us
    broadcast_in_dim x1, other arithmetic, on_device(): grad_image[None]  11.8 us
    reduce_sum x1, other arithmetic, on_device(): centered = pre - jnp.mean(pre, axis=0, keepdims=True)  11.6 us
    ppermute x2, starting transfers between devices, extended(): lax.ppermute(lax.slice_in_dim(block, block.shape[dim] - width, None, axis...  6.68 us
    ppermute x2, starting transfers between devices, extended(): lax.ppermute(lax.slice_in_dim(block, 0, width, axis=dim), axis, backward)  3.84 us
    mul x3, local copies, waits for them, and re-layouts, depthwise(): weight * padded[:, k_row:k_row + strip_w, k_col:k_col + strip_h].astype(j...  2.93 us
  transfers between devices with their start and end apart: 19, of which 8 were waited for; matrix products, arithmetic and copies ran while one was open for 17% of the time, Pallas kernels for 0%

profile of v4, /device:TPU:3, one launch (start us, length us, event | category | flops | bytes accessed | tf_op | source)
XLA Modules:
  0.0 123.8 jit_solution(17120212023040447668)
XLA Ops:
  0.7 0.7 convert_bitcast_fusion
  1.5 1.0 bitcast_multiply_fusion.5
  2.6 4.1 %collective-permute-start = (bf16[96,3,128]{2,1,0:T(4,128)(2,1)S(1)}, bf16[96,3,128]{2,1,0:T(4,128)(2,1)S(1)}, u32[]{:S(2)}, u32[]{:S(2)}) collective-permute-start(bf16[96,3,128]{2,1,0:T(4,128)(2,1)S(1)} %get-tuple-element.80), channel_id=1, source_target_pairs={{0,4},{4,8},{8,12},{12,16},{16,20},{20,24},{24,28},{28,32},{32,36}... | collective-permute-start | bytes 221192 | tf_op jit(solution)/shard_map/ppermute | solution.py:25
  6.8 1.9 %collective-permute-start.1 = (bf16[96,3,128]{2,1,0:T(4,128)(2,1)S(1)}, bf16[96,3,128]{2,1,0:T(4,128)(2,1)S(1)}, u32[]{:S(2)}, u32[]{:S(2)}) collective-permute-start(bf16[96,3,128]{2,1,0:T(4,128)(2,1)S(1)} %get-tuple-element.81), channel_id=1, source_target_pairs={{4,0},{8,4},{12,8},{16,12},{20,16},{24,20},{28,24},{32,28},{36,32}... | collective-permute-start | bytes 221192 | tf_op jit(solution)/shard_map/ppermute | solution.py:28
  8.7 1.0 slice_bitcast_fusion.48
  9.7 1.0 slice_bitcast_fusion.47
  10.7 0.9 slice_bitcast_fusion.46
  11.7 1.2 fusion.19
  12.9 0.8 convert_reduce_fusion.3
  13.7 1.0 select_maximum_fusion.2
  14.8 11.6 %fusion.170 = (f32[16,128]{1,0:T(8,128)S(1)}, f32[96,16,128]{2,1,0:T(8,128)S(1)}) fusion(f32[96]{0:T(128)S(1)} %copy-done.7, bf16[96,22,134]{2,1,0:T(8,128)(2,1)S(1)} %select_maximum_fusion.2, f32[96]{0:T(128)S(1)} %get-tuple-element.132, f32[96]{0:T(128)S(1)} %get-tuple-element.133, f32[96]{0:T(128)S(1)} %get-tuple-element.86, ...), kind=kLoop, calls=%fused_computation.405 | loop fusion | flops 32634880 | bytes 17869568 | tf_op jit(solution)/shard_map/reduce_sum | solution.py:185
  26.9 1.0 fusion.7
  27.8 1.6 %fusion.5 = bf16[384,2048]{0,1:T(8,128)(2,1)S(1)} fusion(f32[2048,384]{1,0:T(8,128)S(1)} %get-tuple-element.135, bf16[96,384]{1,0:T(8,128)(2,1)S(1)} %copy-done.3, bf16[12,8,16,128]{3,2,1,0:T(8,128)(2,1)S(1)} %bitcast.265), kind=kOutput, calls=%fused_computation.59 | convolution fusion | flops 158859264 | bytes 5185536 | tf_op jit(solution)/shard_map/cf,cp->fp/dot_general | solution.py:148
  30.9 1.2 fusion.73
  32.6 7.6 %fusion.149 = (f32[96]{0:T(128)S(1)}, f32[96]{0:T(128)S(1)}, f32[96]{0:T(128)S(1)}, f32[96]{0:T(128)S(1)}, f32[96]{0:T(128)S(1)}, /*index=5*/f32[96]{0:T(128)S(1...) fusion(bf16[96,16,128]{2,1,0:T(8,128)(2,1)S(1)} %fusion.23, ...), kind=kLoop, calls=%fused_computation.270 | loop fusion | flops 10811712 | bytes 7478016 | tf_op jit(solution)/shard_map/reduce_sum | solution.py:125
  40.2 7.6 %fusion.150 = (f32[96]{0:T(128)S(1)}, f32[96]{0:T(128)S(1)}, f32[96]{0:T(128)S(1)}, f32[96]{0:T(128)S(1)}, f32[96]{0:T(128)S(1)}, /*index=5*/f32[96]{0:T(128)S(1...) fusion(bf16[96,16,128]{2,1,0:T(8,128)(2,1)S(1)} %fusion.23, ...), kind=kLoop, calls=%fused_computation.271 | loop fusion | flops 10811712 | bytes 7478016 | tf_op jit(solution)/shard_map/reduce_sum | solution.py:125
  47.8 2.1 %fusion.148 = (f32[96]{0:T(128)S(1)}, f32[96]{0:T(128)S(1)}, f32[96]{0:T(128)S(1)}, f32[96]{0:T(128)S(1)}, f32[96]{0:T(128)S(1)}, /*index=5*/f32[96]{0:T(128)S(1)}) fusion(bf16[96,16,128]{2,1,0:T(8,128)(2,1)S(1)} %fusion.23, bf16[96,22,134]{2,1,0:T(8,128)(2,1)S(1)} %select_maximum_fusion.2), kind=kLoop, calls=%fused_computation.269 | loop fusion | flops 3734976 | bytes 2754816 | tf_op jit(solution)/shard_map/reduce_sum | solution.py:125
  51.1 2.3 %fusion.147 = (f32[96]{0:T(128)S(1)}, f32[96]{0:T(128)S(1)}, f32[96]{0:T(128)S(1)}, f32[96]{0:T(128)S(1)}, f32[96]{0:T(128)S(1)}, /*index=5*/f32[96]{0:T(128)S(1)}, f32[96]{0:T(128)S(1)}, f32[96]{0:T(128)S(1)}) fusion(bf16[96,16,128]{2,1,0:T(8,128)(2,1)S(1)} %fusion.23, bf16[96,3,128]{2,1,0:T(4,128)(2,1)S(1)} %collective-permute-done.1, ...), kind=kLoop, calls=%fused_computation.268 | loop fusion | flops 8060160 | bytes 936960 | tf_op jit(solution)/shard_map/reduce_sum | solution.py:125
  54.0 1.4 %concatenate.35 = f32[79296]{0:T(1024)S(1)} concatenate(f32[73728]{0:T(1024)S(1)} %mul.1410, f32[4704]{0:T(1024)S(1)} %mul.1462, f32[480]{0:T(512)S(1)} %mul.1468, f32[384]{0:T(512)S(1)} %broadcast_multiply_fusion.4), dimensions={0} | concatenate | bytes 634368 | tf_op jit(solution)/shard_map/concatenate | solution.py:53
  55.5 1.8 %collective-permute-start.4 = (f32[155,128]{1,0:T(8,128)S(1)}, f32[155,128]{1,0:T(8,128)S(1)}, u32[]{:S(2)}, u32[]{:S(2)}) collective-permute-start(f32[155,128]{1,0:T(8,128)S(1)} %get-tuple-element.82), channel_id=1, source_target_pairs={{0,4},{4,8},{8,12},{12,0},{16,20},{20,24},{24,28},{28,16},{32,36},... | collective-permute-start | bytes 238088 | tf_op jit(solution)/shard_map/ppermute | solution.py:38
  57.3 3.4 %collective-permute-start.5 = (f32[155,128]{1,0:T(8,128)S(1)}, f32[155,128]{1,0:T(8,128)S(1)}, u32[]{:S(2)}, u32[]{:S(2)}) collective-permute-start(f32[155,128]{1,0:T(8,128)S(1)} %get-tuple-element.84), channel_id=1, source_target_pairs={{0,8},{4,12},{8,0},{12,4},{16,24},{20,28},{24,16},{28,20},{32,40},... | collective-permute-start | bytes 238088 | tf_op jit(solution)/shard_map/ppermute | solution.py:38
  60.7 3.8 %collective-permute-done.5 = f32[155,128]{1,0:T(8,128)S(1)} collective-permute-done((f32[155,128]{1,0:T(8,128)S(1)}, f32[155,128]{1,0:T(8,128)S(1)}, u32[]{:S(2)}, u32[]{:S(2)}) %collective-permute-start.5) | collective-permute-done | bytes 79392 | tf_op jit(solution)/shard_map/ppermute | solution.py:38
  64.5 0.7 collective-permute-done.6
  65.2 1.0 collective-permute-start.7
  66.3 2.6 %collective-permute-start.2 = (bf16[96,3,128]{2,1,0:T(4,128)(2,1)S(1)}, bf16[96,3,128]{2,1,0:T(4,128)(2,1)S(1)}, u32[]{:S(2)}, u32[]{:S(2)}) collective-permute-start(bf16[96,3,128]{2,1,0:T(4,128)(2,1)S(1)} %get-tuple-element.78), channel_id=1, source_target_pairs={{0,4},{4,8},{8,12},{12,16},{16,20},{20,24},{24,28},{28,32},{32,36}... | collective-permute-start | bytes 221192 | tf_op jit(solution)/shard_map/ppermute | solution.py:25
  68.9 1.9 %collective-permute-start.3 = (bf16[96,3,128]{2,1,0:T(4,128)(2,1)S(1)}, bf16[96,3,128]{2,1,0:T(4,128)(2,1)S(1)}, u32[]{:S(2)}, u32[]{:S(2)}) collective-permute-start(bf16[96,3,128]{2,1,0:T(4,128)(2,1)S(1)} %get-tuple-element.79), channel_id=1, source_target_pairs={{4,0},{8,4},{12,8},{16,12},{20,16},{24,20},{28,24},{32,28},{36,32}... | collective-permute-start | bytes 221192 | tf_op jit(solution)/shard_map/ppermute | solution.py:28
  70.8 3.6 %collective-permute-start.8 = (f32[155,128]{1,0:T(8,128)S(1)}, f32[155,128]{1,0:T(8,128)S(1)}, u32[]{:S(2)}, u32[]{:S(2)}) collective-permute-start(f32[155,128]{1,0:T(8,128)S(1)} %get-tuple-element.75), channel_id=1, source_target_pairs={{0,32},{4,36},{8,40},{12,44},{16,48},{20,52},{24,56},{28,60},{32,0... | collective-permute-start | bytes 238088 | tf_op jit(solution)/shard_map/ppermute | solution.py:38
  74.4 3.6 %collective-permute-start.9 = (f32[155,128]{1,0:T(8,128)S(1)}, f32[155,128]{1,0:T(8,128)S(1)}, u32[]{:S(2)}, u32[]{:S(2)}) collective-permute-start(f32[155,128]{1,0:T(8,128)S(1)} %get-tuple-element.75), channel_id=1, source_target_pairs={{0,48},{4,52},{8,56},{12,60},{16,0},{20,4},{24,8},{28,12},{32,16},... | collective-permute-start | bytes 238088 | tf_op jit(solution)/shard_map/ppermute | solution.py:38
  78.1 6.8 %collective-permute-done.9 = f32[155,128]{1,0:T(8,128)S(1)} collective-permute-done((f32[155,128]{1,0:T(8,128)S(1)}, f32[155,128]{1,0:T(8,128)S(1)}, u32[]{:S(2)}, u32[]{:S(2)}) %collective-permute-start.9) | collective-permute-done | bytes 79392 | tf_op jit(solution)/shard_map/ppermute | solution.py:38
  85.0 1.1 collective-permute-start.10
  86.2 1.0 multiply_convert_fusion
  87.2 0.8 collective-permute-start.11
  88.0 1.2 collective-permute-start.12
  89.2 2.9 %collective-permute-done.11 = f32[155,128]{1,0:T(8,128)S(1)} collective-permute-done((f32[155,128]{1,0:T(8,128)S(1)}, f32[155,128]{1,0:T(8,128)S(1)}, u32[]{:S(2)}, u32[]{:S(2)}) %collective-permute-start.11) | collective-permute-done | bytes 79392 | tf_op jit(solution)/shard_map/ppermute | solution.py:38
  92.2 1.4 %collective-permute-start.13 = (f32[155,128]{1,0:T(8,128)S(1)}, f32[155,128]{1,0:T(8,128)S(1)}, u32[]{:S(2)}, u32[]{:S(2)}) collective-permute-start(f32[155,128]{1,0:T(8,128)S(1)} %bitcast.275), channel_id=1, source_target_pairs={{0,1},{1,2},{2,3},{3,0},{4,5},{5,6},{6,7},{7,4},{8,9},{9,10},{10,1... | collective-permute-start | bytes 238088 | tf_op jit(solution)/shard_map/ppermute | solution.py:38
  93.6 1.0 select_maximum_fusion
  94.7 2.7 %collective-permute-start.14 = (f32[155,128]{1,0:T(8,128)S(1)}, f32[155,128]{1,0:T(8,128)S(1)}, u32[]{:S(2)}, u32[]{:S(2)}) collective-permute-start(f32[155,128]{1,0:T(8,128)S(1)} %bitcast.276), channel_id=1, source_target_pairs={{0,2},{1,3},{2,0},{3,1},{4,6},{5,7},{6,4},{7,5},{8,10},{9,11},{10,... | collective-permute-start | bytes 238088 | tf_op jit(solution)/shard_map/ppermute | solution.py:38
  97.4 1.1 collective-permute-start.15
  98.4 1.2 collective-permute-done.14
  99.6 1.1 collective-permute-done.15
  100.8 3.4 %collective-permute-start.16 = (f32[155,128]{1,0:T(8,128)S(1)}, f32[155,128]{1,0:T(8,128)S(1)}, u32[]{:S(2)}, u32[]{:S(2)}) collective-permute-start(f32[155,128]{1,0:T(8,128)S(1)} %fusion.169), channel_id=1, source_target_pairs={{0,4},{4,8},{8,12},{12,0},{16,20},{20,24},{24,28},{28,16},{32,36},... | collective-permute-start | bytes 238088 | tf_op jit(solution)/shard_map/ppermute | solution.py:38
  104.2 2.2 %collective-permute-start.17 = (f32[155,128]{1,0:T(8,128)S(1)}, f32[155,128]{1,0:T(8,128)S(1)}, u32[]{:S(2)}, u32[]{:S(2)}) collective-permute-start(f32[155,128]{1,0:T(8,128)S(1)} %fusion.169), channel_id=1, source_target_pairs={{0,8},{4,12},{8,0},{12,4},{16,24},{20,28},{24,16},{28,20},{32,40},... | collective-permute-start | bytes 238088 | tf_op jit(solution)/shard_map/ppermute | solution.py:38
  106.3 11.8 %fusion.164 = bf16[1,96,16,128]{3,2,1,0:T(8,128)(2,1)} fusion(bf16[96,22,134]{2,1,0:T(8,128)(2,1)S(1)} %select_maximum_fusion, f32[96]{0:T(128)S(1)} %get-tuple-element.85, f32[96]{0:T(128)S(1)} %get-tuple-element.104, f32[96]{0:T(128)S(1)} %get-tuple-element.123, bf16[96,3,128]{2,1,0:T(4,128)(2,1)S(1)} %collective-permute-done.3, ...), kind=kLoop, calls=%fused_computation.314 | loop fusion | flops 33030144 | bytes 17861504 | tf_op jit(solution)/shard_map/broadcast_in_dim | solution.py:231
  118.2 0.7 dynamic_update_slice.61
  118.9 0.7 dynamic_update_slice.62
  120.0 0.7 dynamic_update_slice.64
  121.5 0.8 reshape.231
  122.4 0.7 copy.19
  (92 shorter events, 7.0 us)
Async XLA Ops:
  0.6 26.2 %copy-start = (bf16[96,384]{1,0:T(8,128)(2,1)S(1)}, bf16[96,384]{1,0:T(8,128)(2,1)}, u32[]{:S(2)}) copy-start(bf16[96,384]{1,0:T(8,128)(2,1)} %param.19) | copy-start | bytes 221188
  0.6 14.1 %copy-start.7 = (f32[96]{0:T(128)S(1)}, f32[96]{0:T(128)}, u32[]{:S(2)}) copy-start(f32[96]{0:T(128)} %param.16) | copy-start | bytes 1156
  2.6 11.1 %collective-permute-start = (bf16[96,3,128]{2,1,0:T(4,128)(2,1)S(1)}, bf16[96,3,128]{2,1,0:T(4,128)(2,1)S(1)}, u32[]{:S(2)}, u32[]{:S(2)}) collective-permute-start(bf16[96,3,128]{2,1,0:T(4,128)(2,1)S(1)} %get-tuple-element.80), channel_id=1, source_target_pairs={{0,4},{4,8},{8,12},{12,16},{16,20},{20,24},{24,28},{28,32},{32,36}... | collective-permute-start | bytes 221192 | tf_op jit(solution)/shard_map/ppermute | solution.py:25
  6.8 7.0 %collective-permute-start.1 = (bf16[96,3,128]{2,1,0:T(4,128)(2,1)S(1)}, bf16[96,3,128]{2,1,0:T(4,128)(2,1)S(1)}, u32[]{:S(2)}, u32[]{:S(2)}) collective-permute-start(bf16[96,3,128]{2,1,0:T(4,128)(2,1)S(1)} %get-tuple-element.81), channel_id=1, source_target_pairs={{4,0},{8,4},{12,8},{16,12},{20,16},{24,20},{28,24},{32,28},{36,32}... | collective-permute-start | bytes 221192 | tf_op jit(solution)/shard_map/ppermute | solution.py:28
  14.8 11.8 %copy-start.4 = (f32[96]{0:T(128)S(1)}, f32[96]{0:T(128)}, u32[]{:S(2)}) copy-start(f32[96]{0:T(128)} %param.17) | copy-start | bytes 1156
  14.8 11.7 %copy-start.8 = (f32[96]{0:T(128)S(1)}, f32[96]{0:T(128)}, u32[]{:S(2)}) copy-start(f32[96]{0:T(128)} %param.18) | copy-start | bytes 1156
  14.8 12.0 %copy-start.6 = (f32[384]{0:T(512)S(1)}, f32[384]{0:T(512)}, u32[]{:S(2)}) copy-start(f32[384]{0:T(512)} %param.20) | copy-start | bytes 4612
  26.8 1.0 copy-start.3
  29.5 0.7 copy-start.9
  29.5 1.4 %copy-start.1 = (bf16[1,96,16,128]{3,2,1,0:T(8,128)(2,1)S(1)}, bf16[1,96,16,128]{3,2,1,0:T(8,128)(2,1)}, u32[]{:S(2)}) copy-start(bf16[1,96,16,128]{3,2,1,0:T(8,128)(2,1)} %param.13) | copy-start | bytes 1179652
  54.0 32.2 %copy-start.2 = (bf16[1,96,16,128]{3,2,1,0:T(8,128)(2,1)S(1)}, bf16[1,96,16,128]{3,2,1,0:T(8,128)(2,1)}, u32[]{:S(2)}) copy-start(bf16[1,96,16,128]{3,2,1,0:T(8,128)(2,1)} %param.12) | copy-start | bytes 1179652
  54.0 32.1 %copy-start.5 = (f32[96]{0:T(128)S(1)}, f32[96]{0:T(128)}, u32[]{:S(2)}) copy-start(f32[96]{0:T(128)} %param.23) | copy-start | bytes 1156
  55.5 5.2 %collective-permute-start.4 = (f32[155,128]{1,0:T(8,128)S(1)}, f32[155,128]{1,0:T(8,128)S(1)}, u32[]{:S(2)}, u32[]{:S(2)}) collective-permute-start(f32[155,128]{1,0:T(8,128)S(1)} %get-tuple-element.82), channel_id=1, source_target_pairs={{0,4},{4,8},{8,12},{12,0},{16,20},{20,24},{24,28},{28,16},{32,36},... | collective-permute-start | bytes 238088 | tf_op jit(solution)/shard_map/ppermute | solution.py:38
  57.3 7.1 %collective-permute-start.5 = (f32[155,128]{1,0:T(8,128)S(1)}, f32[155,128]{1,0:T(8,128)S(1)}, u32[]{:S(2)}, u32[]{:S(2)}) collective-permute-start(f32[155,128]{1,0:T(8,128)S(1)} %get-tuple-element.84), channel_id=1, source_target_pairs={{0,8},{4,12},{8,0},{12,4},{16,24},{20,28},{24,16},{28,20},{32,40},... | collective-permute-start | bytes 238088 | tf_op jit(solution)/shard_map/ppermute | solution.py:38
  60.7 4.5 %collective-permute-start.6 = (f32[155,128]{1,0:T(8,128)S(1)}, f32[155,128]{1,0:T(8,128)S(1)}, u32[]{:S(2)}, u32[]{:S(2)}) collective-permute-start(f32[155,128]{1,0:T(8,128)S(1)} %get-tuple-element.83), channel_id=1, source_target_pairs={{0,12},{4,0},{8,4},{12,8},{16,28},{20,16},{24,20},{28,24},{32,44},... | collective-permute-start | bytes 238088 | tf_op jit(solution)/shard_map/ppermute | solution.py:38
  65.2 12.8 %collective-permute-start.7 = (f32[155,128]{1,0:T(8,128)S(1)}, f32[155,128]{1,0:T(8,128)S(1)}, u32[]{:S(2)}, u32[]{:S(2)}) collective-permute-start(f32[155,128]{1,0:T(8,128)S(1)} %get-tuple-element.75), channel_id=1, source_target_pairs={{0,16},{4,20},{8,24},{12,28},{16,32},{20,36},{24,40},{28,44},{32,4... | collective-permute-start | bytes 238088 | tf_op jit(solution)/shard_map/ppermute | solution.py:38
  66.3 27.3 %collective-permute-start.2 = (bf16[96,3,128]{2,1,0:T(4,128)(2,1)S(1)}, bf16[96,3,128]{2,1,0:T(4,128)(2,1)S(1)}, u32[]{:S(2)}, u32[]{:S(2)}) collective-permute-start(bf16[96,3,128]{2,1,0:T(4,128)(2,1)S(1)} %get-tuple-element.78), channel_id=1, source_target_pairs={{0,4},{4,8},{8,12},{12,16},{16,20},{20,24},{24,28},{28,32},{32,36}... | collective-permute-start | bytes 221192 | tf_op jit(solution)/shard_map/ppermute | solution.py:25
  68.9 24.7 %collective-permute-start.3 = (bf16[96,3,128]{2,1,0:T(4,128)(2,1)S(1)}, bf16[96,3,128]{2,1,0:T(4,128)(2,1)S(1)}, u32[]{:S(2)}, u32[]{:S(2)}) collective-permute-start(bf16[96,3,128]{2,1,0:T(4,128)(2,1)S(1)} %get-tuple-element.79), channel_id=1, source_target_pairs={{4,0},{8,4},{12,8},{16,12},{20,16},{24,20},{28,24},{32,28},{36,32}... | collective-permute-start | bytes 221192 | tf_op jit(solution)/shard_map/ppermute | solution.py:28
  70.8 7.3 %collective-permute-start.8 = (f32[155,128]{1,0:T(8,128)S(1)}, f32[155,128]{1,0:T(8,128)S(1)}, u32[]{:S(2)}, u32[]{:S(2)}) collective-permute-start(f32[155,128]{1,0:T(8,128)S(1)} %get-tuple-element.75), channel_id=1, source_target_pairs={{0,32},{4,36},{8,40},{12,44},{16,48},{20,52},{24,56},{28,60},{32,0... | collective-permute-start | bytes 238088 | tf_op jit(solution)/shard_map/ppermute | solution.py:38
  74.4 10.5 %collective-permute-start.9 = (f32[155,128]{1,0:T(8,128)S(1)}, f32[155,128]{1,0:T(8,128)S(1)}, u32[]{:S(2)}, u32[]{:S(2)}) collective-permute-start(f32[155,128]{1,0:T(8,128)S(1)} %get-tuple-element.75), channel_id=1, source_target_pairs={{0,48},{4,52},{8,56},{12,60},{16,0},{20,4},{24,8},{28,12},{32,16},... | collective-permute-start | bytes 238088 | tf_op jit(solution)/shard_map/ppermute | solution.py:38
  85.0 4.2 %collective-permute-start.10 = (f32[155,128]{1,0:T(8,128)S(1)}, f32[155,128]{1,0:T(8,128)S(1)}, u32[]{:S(2)}, u32[]{:S(2)}) collective-permute-start(f32[155,128]{1,0:T(8,128)S(1)} %bitcast.278), channel_id=1, source_target_pairs={{0,64},{4,68},{8,72},{12,76},{16,80},{20,84},{24,88},{28,92},{32,9... | collective-permute-start | bytes 238088 | tf_op jit(solution)/shard_map/ppermute | solution.py:38
  87.2 4.9 %collective-permute-start.11 = (f32[155,128]{1,0:T(8,128)S(1)}, f32[155,128]{1,0:T(8,128)S(1)}, u32[]{:S(2)}, u32[]{:S(2)}) collective-permute-start(f32[155,128]{1,0:T(8,128)S(1)} %bitcast.279), channel_id=1, source_target_pairs={{0,128},{4,132},{8,136},{12,140},{16,144},{20,148},{24,152},{28,15... | collective-permute-start | bytes 238088 | tf_op jit(solution)/shard_map/ppermute | solution.py:38
  88.0 4.2 %collective-permute-start.12 = (f32[155,128]{1,0:T(8,128)S(1)}, f32[155,128]{1,0:T(8,128)S(1)}, u32[]{:S(2)}, u32[]{:S(2)}) collective-permute-start(f32[155,128]{1,0:T(8,128)S(1)} %bitcast.280), channel_id=1, source_target_pairs={{0,192},{4,196},{8,200},{12,204},{16,208},{20,212},{24,216},{28,22... | collective-permute-start | bytes 238088 | tf_op jit(solution)/shard_map/ppermute | solution.py:38
  92.2 6.2 %collective-permute-start.13 = (f32[155,128]{1,0:T(8,128)S(1)}, f32[155,128]{1,0:T(8,128)S(1)}, u32[]{:S(2)}, u32[]{:S(2)}) collective-permute-start(f32[155,128]{1,0:T(8,128)S(1)} %bitcast.275), channel_id=1, source_target_pairs={{0,1},{1,2},{2,3},{3,0},{4,5},{5,6},{6,7},{7,4},{8,9},{9,10},{10,1... | collective-permute-start | bytes 238088 | tf_op jit(solution)/shard_map/ppermute | solution.py:38
  94.7 4.9 %collective-permute-start.14 = (f32[155,128]{1,0:T(8,128)S(1)}, f32[155,128]{1,0:T(8,128)S(1)}, u32[]{:S(2)}, u32[]{:S(2)}) collective-permute-start(f32[155,128]{1,0:T(8,128)S(1)} %bitcast.276), channel_id=1, source_target_pairs={{0,2},{1,3},{2,0},{3,1},{4,6},{5,7},{6,4},{7,5},{8,10},{9,11},{10,... | collective-permute-start | bytes 238088 | tf_op jit(solution)/shard_map/ppermute | solution.py:38
  97.4 3.3 %collective-permute-start.15 = (f32[155,128]{1,0:T(8,128)S(1)}, f32[155,128]{1,0:T(8,128)S(1)}, u32[]{:S(2)}, u32[]{:S(2)}) collective-permute-start(f32[155,128]{1,0:T(8,128)S(1)} %bitcast.277), channel_id=1, source_target_pairs={{0,3},{1,0},{2,1},{3,2},{4,7},{5,4},{6,5},{7,6},{8,11},{9,8},{10,9... | collective-permute-start | bytes 238088 | tf_op jit(solution)/shard_map/ppermute | solution.py:38
  100.8 18.1 %collective-permute-start.16 = (f32[155,128]{1,0:T(8,128)S(1)}, f32[155,128]{1,0:T(8,128)S(1)}, u32[]{:S(2)}, u32[]{:S(2)}) collective-permute-start(f32[155,128]{1,0:T(8,128)S(1)} %fusion.169), channel_id=1, source_target_pairs={{0,4},{4,8},{8,12},{12,0},{16,20},{20,24},{24,28},{28,16},{32,36},... | collective-permute-start | bytes 238088 | tf_op jit(solution)/shard_map/ppermute | solution.py:38
  104.2 15.4 %collective-permute-start.17 = (f32[155,128]{1,0:T(8,128)S(1)}, f32[155,128]{1,0:T(8,128)S(1)}, u32[]{:S(2)}, u32[]{:S(2)}) collective-permute-start(f32[155,128]{1,0:T(8,128)S(1)} %fusion.169), channel_id=1, source_target_pairs={{0,8},{4,12},{8,0},{12,4},{16,24},{20,28},{24,16},{28,20},{32,40},... | collective-permute-start | bytes 238088 | tf_op jit(solution)/shard_map/ppermute | solution.py:38
  106.3 13.7 %collective-permute-start.18 = (f32[155,128]{1,0:T(8,128)S(1)}, f32[155,128]{1,0:T(8,128)S(1)}, u32[]{:S(2)}, u32[]{:S(2)}) collective-permute-start(f32[155,128]{1,0:T(8,128)S(1)} %fusion.169), channel_id=1, source_target_pairs={{0,12},{4,0},{8,4},{12,8},{16,28},{20,16},{24,20},{28,24},{32,44},... | collective-permute-start | bytes 238088 | tf_op jit(solution)/shard_map/ppermute | solution.py:38
